TPU v7x, 256 devices: a whole 4x4x8 slice. The times are simulated.
256 devices in a mesh: ctx: 64 (over x, y_lo, z), rep: 4 (over y_hi, core).
Axes of the slice: x: 4, y: 4 (y_hi: 2, y_lo: 2; y = y_hi * 2 + y_lo), z: 8, core: 2. Of those that a mesh axis runs over, the one named last changes fastest.
Arguments:
- tokens: bfloat16 [4, 8192, 2880], P('rep', 'ctx'), may hold values from -6 to 6
- router_w: bfloat16 [2880, 32], replicated, may hold values from -0.109375 to 0.109375
- router_b: float32 [32], replicated, may hold values from -4 to 4
- hidden: bfloat16 [4, 8192, 4, 1536], P('rep', 'ctx'), may hold values from -6 to 6
- teacher_idx: int32 [4, 8192, 4], P('rep', 'ctx'), may hold values from 0 to 31, all different within a row
- merge_map: int32 [32], replicated, may hold values from 0 to 15, as said below
- merge_coef: float32 [32], replicated, may hold values from 0.3 to 1.5
- source_w: bfloat16 [32, 1536, 1536], P(None, 'ctx'), may hold values from -0.15625 to 0.15625
- out_grad: bfloat16 [4, 8192, 1536], P('rep', 'ctx'), may hold values from -6 to 6
Outputs:
- mixed: bfloat16 [4, 8192, 1536], P('rep', 'ctx')
- hidden_grad: bfloat16 [4, 8192, 4, 1536], P('rep', 'ctx')
- token_grad: bfloat16 [4, 8192, 2880], P('rep', 'ctx')
- router_w_grad: float32 [2880, 32], replicated
- router_b_grad: float32 [32], replicated
- coef_grad: float32 [32], replicated
- source_w_grad: float32 [32, 1536, 1536], P(None, 'ctx', 'rep')
Inputs may be any that keep to these rules, and one draw needn't show every extreme that they name: `teacher_idx`: each token names 4 different experts. `merge_map`: each of the 16 combinations takes exactly two of the 32 experts.
All inputs are finite; a program needn't handle non-finite values.
Results may differ from a plain program's by a relative error of at most 0.0064.
Values may be sent and summed in bfloat16 or wider, within the bound.
A program may use at most 128 MiB of HBM per device.

v0:
```python
import math

import jax
import jax.numpy as jnp
from jax import lax
from jax.sharding import PartitionSpec as P

MERGED = 16


def expert_rows(rows_hidden, rows_grad, rows_member, lane_weights):
    row_count = rows_hidden.shape[0]
    out_rows = jnp.zeros((row_count, lane_weights.shape[1]), jnp.float32)
    back_rows = jnp.zeros((row_count, lane_weights.shape[2]), jnp.float32)
    weight = lane_weights[0]
    selected = (rows_member == 0)[:, None]
    forward = lax.dot_general(
        rows_hidden, weight, (((1,), (1,)), ((), ())), preferred_element_type=jnp.float32
    )
    out_rows = jnp.where(selected, forward, out_rows)
    backward = jnp.dot(rows_grad, weight, preferred_element_type=jnp.float32)
    back_rows = jnp.where(selected, backward, back_rows)
    masked = jnp.where(selected, rows_grad, jnp.zeros_like(rows_grad))
    grad_list = [
        lax.dot_general(
            masked, rows_hidden, (((0,), (0,)), ((), ())), preferred_element_type=jnp.float32
        )
    ]
    return (out_rows, back_rows, jnp.stack(grad_list))


def on_device(
    tokens, router_w, router_b, hidden, teacher_idx, merge_map, merge_coef, source_w, out_grad
):
    ctx_count = lax.axis_size("ctx")
    rep_count = lax.axis_size("rep")
    tok_count = tokens.shape[1]
    feature_count = tokens.shape[2]
    top_count = teacher_idx.shape[2]
    hidden_width = hidden.shape[3]
    out_width = out_grad.shape[2]
    source_count = router_w.shape[1]
    row_share = source_w.shape[1]
    per_lane = max(1, MERGED // ctx_count)
    copies = max(1, ctx_count // MERGED)
    capacity = 5 * tok_count * top_count // (4 * ctx_count)
    slot_count = tok_count * top_count
    grad_scale = 1.0 / math.sqrt(tok_count * ctx_count * rep_count)
    flat_x = tokens.reshape(tok_count, feature_count)
    logits = jnp.dot(flat_x, router_w, preferred_element_type=jnp.float32) + router_b
    choice_ids = teacher_idx.reshape(tok_count, top_count)
    pick_table = choice_ids[:, :, None] == jnp.arange(source_count, dtype=jnp.int32)[None, None, :]
    pick_float = pick_table.astype(jnp.float32)
    chosen = jnp.sum(pick_float * logits[:, None, :], axis=2)
    raised = jnp.exp(chosen)
    gate_probs = raised / jnp.sum(raised, axis=1, keepdims=True)
    merged_id = jnp.sum(jnp.where(pick_table, merge_map[None, None, :], 0), axis=2)
    position = lax.axis_index("ctx") * tok_count + jnp.arange(tok_count, dtype=jnp.int32)
    lane_id = merged_id // per_lane * copies + (position % copies)[:, None]
    member_id = (merged_id % per_lane).reshape(-1)
    lane_flat = lane_id.reshape(-1)
    onehot = (lane_flat[:, None] == jnp.arange(ctx_count, dtype=jnp.int32)[None, :]).astype(
        jnp.int32
    )
    before = jnp.cumsum(onehot, axis=0) - onehot
    slot_rank = jnp.sum(before * onehot, axis=1)
    is_kept = slot_rank < capacity
    slot_index = jnp.where(is_kept, lane_flat * capacity + slot_rank, ctx_count * capacity)
    slot_source = (
        jnp.full((ctx_count * capacity + 1,), slot_count, jnp.int32)
        .at[slot_index]
        .set(jnp.arange(slot_count, dtype=jnp.int32))[: ctx_count * capacity]
    )
    slot_grad = (gate_probs[:, :, None] * out_grad.reshape(tok_count, 1, out_width)).astype(
        jnp.bfloat16
    )
    pad_hidden = jnp.concatenate(
        [hidden.reshape(slot_count, hidden_width), jnp.zeros((1, hidden_width), jnp.bfloat16)],
        axis=0,
    )
    pad_grad = jnp.concatenate(
        [slot_grad.reshape(slot_count, out_width), jnp.zeros((1, out_width), jnp.bfloat16)], axis=0
    )
    pad_member = jnp.concatenate([member_id, jnp.zeros((1,), jnp.int32)], axis=0)
    send_hidden = pad_hidden[slot_source].reshape(ctx_count, capacity, hidden_width)
    send_grad = pad_grad[slot_source].reshape(ctx_count, capacity, out_width)
    send_member = pad_member[slot_source].reshape(ctx_count, capacity)
    lane_group = lax.axis_index("ctx") // copies
    same_group = merge_map[:, None] == merge_map[None, :]
    earlier = jnp.arange(source_count)[:, None] > jnp.arange(source_count)[None, :]
    member_rank = jnp.sum((same_group & earlier).astype(jnp.int32), axis=1)
    source_order = (
        jnp.zeros((source_count,), jnp.int32)
        .at[2 * merge_map + member_rank]
        .set(jnp.arange(source_count, dtype=jnp.int32))
    )
    picked = source_w[source_order].reshape(
        MERGED // per_lane, 2 * per_lane, row_share, hidden_width
    )
    outgoing = jnp.repeat(picked, copies, axis=0)
    arrived = lax.all_to_all(outgoing, "ctx", split_axis=0, concat_axis=2, tiled=True)
    coef_table = merge_coef[source_order].reshape(MERGED // per_lane, per_lane, 2)
    pair_coef = lax.dynamic_index_in_dim(coef_table, lane_group, 0, keepdims=False)
    lane_weights = (
        pair_coef[:, 0, None, None] * arrived[:, 0].astype(jnp.float32)
        + pair_coef[:, 1, None, None] * arrived[:, 1].astype(jnp.float32)
    ).astype(jnp.bfloat16)
    recv_hidden, recv_grad, recv_member = (
        lax.all_to_all(send_hidden, "ctx", split_axis=0, concat_axis=0, tiled=True),
        lax.all_to_all(send_grad, "ctx", split_axis=0, concat_axis=0, tiled=True),
        lax.all_to_all(send_member, "ctx", split_axis=0, concat_axis=0, tiled=True),
    )
    out_rows, back_rows, lane_grads = expert_rows(
        recv_hidden.reshape(-1, hidden_width),
        recv_grad.reshape(-1, out_width),
        recv_member.reshape(-1),
        lane_weights,
    )
    home_out, home_back = (
        lax.all_to_all(
            out_rows.astype(jnp.bfloat16).reshape(ctx_count, capacity, out_width),
            "ctx",
            split_axis=0,
            concat_axis=0,
            tiled=True,
        ),
        lax.all_to_all(
            back_rows.astype(jnp.bfloat16).reshape(ctx_count, capacity, hidden_width),
            "ctx",
            split_axis=0,
            concat_axis=0,
            tiled=True,
        ),
    )
    slot_out = jnp.concatenate(
        [home_out.reshape(-1, out_width), jnp.zeros((1, out_width), jnp.bfloat16)], axis=0
    )[slot_index].reshape(tok_count, top_count, out_width)
    hidden_grad = jnp.concatenate(
        [home_back.reshape(-1, hidden_width), jnp.zeros((1, hidden_width), jnp.bfloat16)], axis=0
    )[slot_index].reshape(1, tok_count, top_count, hidden_width)
    mixed = (
        jnp.sum(gate_probs[:, :, None] * slot_out.astype(jnp.float32), axis=1)
        .astype(jnp.bfloat16)
        .reshape(1, tok_count, out_width)
    )
    score_grad = jnp.einsum(
        "td,tkd->tk",
        out_grad.reshape(tok_count, out_width),
        slot_out,
        preferred_element_type=jnp.float32,
    )
    chosen_grad = gate_probs * (
        score_grad - jnp.sum(gate_probs * score_grad, axis=1, keepdims=True)
    )
    logit_grad = jnp.sum(pick_float * chosen_grad[:, :, None], axis=1)
    logit_half = logit_grad.astype(jnp.bfloat16)
    token_grad = (
        lax.dot_general(
            logit_half, router_w, (((1,), (1,)), ((), ())), preferred_element_type=jnp.float32
        )
        .astype(jnp.bfloat16)
        .reshape(1, tok_count, feature_count)
    )
    part_router_w = lax.dot_general(
        flat_x, logit_half, (((0,), (0,)), ((), ())), preferred_element_type=jnp.float32
    )
    part_router_b = jnp.sum(logit_grad, axis=0)
    arrived_grads = lax.all_to_all(
        lane_grads.reshape(per_lane, ctx_count, row_share, hidden_width),
        "ctx",
        split_axis=1,
        concat_axis=0,
        tiled=True,
    )
    merged_grad = (
        arrived_grads.reshape(MERGED // per_lane, copies, per_lane, row_share, hidden_width)
        .sum(axis=1)
        .reshape(MERGED, row_share, hidden_width)
    )
    source_grad = merged_grad[merge_map]
    coef_part = jnp.einsum(
        "edf,edf->e", source_grad, source_w.astype(jnp.float32), precision=lax.Precision.HIGHEST
    )
    summed = lax.psum_scatter(
        source_grad * merge_coef[:, None, None], "rep", scatter_dimension=2, tiled=True
    )
    source_w_grad = summed * grad_scale
    router_sum, bias_sum, coef_sum = lax.psum(
        (part_router_w, part_router_b, coef_part), ("ctx", "rep")
    )
    return (
        mixed,
        hidden_grad,
        token_grad,
        router_sum * grad_scale,
        bias_sum * grad_scale,
        coef_sum * grad_scale,
        source_w_grad,
    )


def solution(mesh):
    in_specs = (
        P("rep", "ctx", None),
        P(),
        P(),
        P("rep", "ctx", None, None),
        P("rep", "ctx", None),
        P(),
        P(),
        P(None, "ctx", None),
        P("rep", "ctx", None),
    )
    out_specs = (
        P("rep", "ctx", None),
        P("rep", "ctx", None, None),
        P("rep", "ctx", None),
        P(),
        P(),
        P(),
        P(None, "ctx", "rep"),
    )
    return jax.shard_map(
        on_device, mesh=mesh, in_specs=in_specs, out_specs=out_specs, check_vma=False
    )
```

profile of v0, /device:TPU:1, one launch (start us, length us, event | category | flops | bytes accessed | tf_op | source)
XLA Modules:
  0.0 1014.5 jit_solution(12828136133311541424)
XLA Ops:
  11.4 2.4 scatter_custom_fusion
  13.9 2.8 gather_fusion
  17.5 13.5 %all-to-all-start = ((s32[64,1,10]{2,1,0:T(1,128)}), s32[64,1,10]{2,1,0:T(1,128)S(1)}, u32[]{:S(2)}, u32[]{:S(2)}) async-start(s32[64,1,10]{2,1,0:T(1,128)} %bitcast.5), calls=%async_computation | async-start | bytes 65536 | tf_op jit(solution)/shard_map/all_to_all | solution.py:111
  33.8 3.7 gather_fusion.1
  37.5 4.2 reshape.274
  41.7 11.1 %all-to-all-start.1 = ((bf16[64,10,1536]{2,1,0:T(8,128)(2,1)}), bf16[64,10,1536]{2,1,0:T(8,128)(2,1)}, u32[]{:S(2)}, u32[]{:S(2)}) async-start(bf16[64,10,1536]{2,1,0:T(8,128)(2,1)} %reshape.274), calls=%async_computation.1 | async-start | bytes 6291456 | tf_op jit(solution)/shard_map/all_to_all | solution.py:109
  53.7 2.1 gather_fusion.3
  55.8 66.0 %all-to-all-done.1 = bf16[64,10,1536]{2,1,0:T(8,128)(2,1)} async-done(((bf16[64,10,1536]{2,1,0:T(8,128)(2,1)}), bf16[64,10,1536]{2,1,0:T(8,128)(2,1)}, u32[]{:S(2)}, u32[]{:S(2)}) %all-to-all-start.1) | async-done | bytes 1966112 | tf_op jit(solution)/shard_map/all_to_all | solution.py:109
  121.8 6.5 broadcast_in_dim.85
  128.3 10.5 %all-to-all-start.2 = ((bf16[64,2,24,1536]{3,2,1,0:T(8,128)(2,1)}), bf16[64,2,24,1536]{3,2,1,0:T(8,128)(2,1)}, u32[]{:S(2)}, u32[]{:S(2)}) async-start(bf16[64,2,24,1536]{3,2,1,0:T(8,128)(2,1)} %bitcast.77), calls=%async_computation.2 | async-start | bytes 18874368 | tf_op jit(solution)/shard_map/all_to_all | solution.py:101
  140.5 2.9 reshape.275
  143.4 199.7 %all-to-all-done.2 = bf16[64,2,24,1536]{3,2,1,0:T(8,128)(2,1)} async-done(((bf16[64,2,24,1536]{3,2,1,0:T(8,128)(2,1)}), bf16[64,2,24,1536]{3,2,1,0:T(8,128)(2,1)}, u32[]{:S(2)}, u32[]{:S(2)}) %all-to-all-start.2) | async-done | bytes 9437216 | tf_op jit(solution)/shard_map/all_to_all | solution.py:101
  343.1 8.1 copy.44
  351.1 9.8 select_convert_fusion.1
  360.9 4.2 reshape.279
  365.1 11.4 %all-to-all-start.3 = ((bf16[64,10,1536]{2,1,0:T(8,128)(2,1)}), bf16[64,10,1536]{2,1,0:T(8,128)(2,1)}, u32[]{:S(2)}, u32[]{:S(2)}) async-start(bf16[64,10,1536]{2,1,0:T(8,128)(2,1)} %reshape.279), calls=%async_computation.3 | async-start | bytes 6291456 | tf_op jit(solution)/shard_map/all_to_all | solution.py:120
  376.7 2.2 mul.170
  378.9 5.0 mul.171
  384.2 61.5 %all-to-all-done.3 = bf16[64,10,1536]{2,1,0:T(8,128)(2,1)} async-done(((bf16[64,10,1536]{2,1,0:T(8,128)(2,1)}), bf16[64,10,1536]{2,1,0:T(8,128)(2,1)}, u32[]{:S(2)}, u32[]{:S(2)}) %all-to-all-start.3) | async-done | bytes 1966112 | tf_op jit(solution)/shard_map/all_to_all | solution.py:120
  445.7 4.3 reshape.280
  451.6 2.9 gather_fusion.4
  454.6 2.9 reshape.281
  457.5 1.8 fusion.2
  459.7 2.1 multiply_convert_fusion
  461.9 3.7 gather_fusion.5
  465.7 4.2 reshape.283
  469.9 11.0 %all-to-all-start.4 = ((bf16[64,10,1536]{2,1,0:T(8,128)(2,1)}), bf16[64,10,1536]{2,1,0:T(8,128)(2,1)}, u32[]{:S(2)}, u32[]{:S(2)}) async-start(bf16[64,10,1536]{2,1,0:T(8,128)(2,1)} %reshape.283), calls=%async_computation.4 | async-start | bytes 6291456 | tf_op jit(solution)/shard_map/all_to_all | solution.py:110
  480.8 4.2 reshape.380
  485.1 64.7 %all-to-all-done.4 = bf16[64,10,1536]{2,1,0:T(8,128)(2,1)} async-done(((bf16[64,10,1536]{2,1,0:T(8,128)(2,1)}), bf16[64,10,1536]{2,1,0:T(8,128)(2,1)}, u32[]{:S(2)}, u32[]{:S(2)}) %all-to-all-start.4) | async-done | bytes 1966112 | tf_op jit(solution)/shard_map/all_to_all | solution.py:110
  549.8 2.9 reshape.284
  554.5 4.0 copy.46
  558.4 9.7 convolution_bitcast_fusion
  568.1 10.7 %all-to-all-start.6 = ((f32[1,64,24,1536]{3,2,0,1:T(8,128)}), f32[1,64,24,1536]{3,2,0,1:T(8,128)}, u32[]{:S(2)}, u32[]{:S(2)}) async-start(f32[1,64,24,1536]{3,2,0,1:T(8,128)} %convolution_bitcast_fusion), calls=%async_computation.6 | async-start | bytes 18874368 | tf_op jit(solution)/shard_map/all_to_all | solution.py:168
  580.2 205.3 %all-to-all-done.6 = f32[1,64,24,1536]{3,2,0,1:T(8,128)} async-done(((f32[1,64,24,1536]{3,2,0,1:T(8,128)}), f32[1,64,24,1536]{3,2,0,1:T(8,128)}, u32[]{:S(2)}, u32[]{:S(2)}) %all-to-all-start.6) | async-done | bytes 9437216 | tf_op jit(solution)/shard_map/all_to_all | solution.py:168
  785.5 5.2 reduce_sum.102
  790.7 3.1 gather_fusion.7
  793.8 6.3 broadcast_multiply_fusion
  801.6 9.6 select_convert_fusion
  811.3 4.2 reshape.285
  815.5 12.3 %all-to-all-start.5 = ((bf16[64,10,1536]{2,1,0:T(8,128)(2,1)}), bf16[64,10,1536]{2,1,0:T(8,128)(2,1)}, u32[]{:S(2)}, u32[]{:S(2)}) async-start(bf16[64,10,1536]{2,1,0:T(8,128)(2,1)} %reshape.285), calls=%async_computation.5 | async-start | bytes 6291456 | tf_op jit(solution)/shard_map/all_to_all | solution.py:127
  829.1 3.1 multiply_reduce_fusion.1
  832.1 82.0 %all-reduce.7.cloned.1.call-done = f32[2880,32]{0,1:T(8,128)} async-done(((f32[2880,32]{0,1:T(8,128)}), f32[2880,32]{0,1:T(8,128)}) %all-reduce.7.cloned.1.call-update) | async-done | bytes 368656 | tf_op jit(solution)/shard_map/psum | solution.py:188
  914.1 1.8 broadcast_multiply_fusion.2
  915.9 4.2 reshape.286
  921.8 3.0 gather_fusion.6
  924.7 3.8 reshape.287
  928.6 75.3 %all-reduce.4 = (f32[32]{0:T(128)S(1)}, f32[32]{0:T(128)S(1)}) all-reduce(f32[32]{0:T(128)S(1)} %get-tuple-element.7, f32[32]{0:T(128)S(1)} %get-tuple-element.16), channel_id=1, replica_groups=mesh['ctx'=64,'rep'=4] {'ctx','rep'}, use_global_device_ids=true, to_apply=%region_14.15 | all-reduce | flops 64 | bytes 512 | tf_op jit(solution)/shard_map/psum | solution.py:188
  1004.4 2.4 broadcast_multiply_fusion.1
  (93 shorter events, 20.1 us)
Async XLA Ops:
  8.0 375.8 %copy-start = (bf16[1,128,2880]{1,2,0:T(8,128)(2,1)S(1)}, bf16[1,128,2880]{1,2,0:T(8,128)(2,1)}, u32[]{:S(2)}) copy-start(bf16[1,128,2880]{1,2,0:T(8,128)(2,1)} %param.9) | copy-start | bytes 2211844
  10.8 20.2 %copy-start.7 = (bf16[1,128,4,1536]{3,2,1,0:T(4,128)(2,1)S(1)}, bf16[1,128,4,1536]{3,2,1,0:T(4,128)(2,1)}, u32[]{:S(2)}) copy-start(bf16[1,128,4,1536]{3,2,1,0:T(4,128)(2,1)} %param.12) | copy-start | bytes 4718596
  17.5 24.2 %all-to-all-start = ((s32[64,1,10]{2,1,0:T(1,128)}), s32[64,1,10]{2,1,0:T(1,128)S(1)}, u32[]{:S(2)}, u32[]{:S(2)}) async-start(s32[64,1,10]{2,1,0:T(1,128)} %bitcast.5), calls=%async_computation | async-start | bytes 65536 | tf_op jit(solution)/shard_map/all_to_all | solution.py:111
  41.7 11.1 %copy-start.12 = (s32[32]{0:T(128)S(1)}, s32[32]{0:T(128)}, u32[]{:S(2)}) copy-start(s32[32]{0:T(128)} %param.14) | copy-start | bytes 388
  41.7 12.0 %copy-start.2 = (bf16[32,24,1536]{2,1,0:T(8,128)(2,1)S(1)}, bf16[32,24,1536]{2,1,0:T(8,128)(2,1)}, u32[]{:S(2)}) copy-start(bf16[32,24,1536]{2,1,0:T(8,128)(2,1)} %param.16) | copy-start | bytes 7077892
  41.7 80.1 %all-to-all-start.1 = ((bf16[64,10,1536]{2,1,0:T(8,128)(2,1)}), bf16[64,10,1536]{2,1,0:T(8,128)(2,1)}, u32[]{:S(2)}, u32[]{:S(2)}) async-start(bf16[64,10,1536]{2,1,0:T(8,128)(2,1)} %reshape.274), calls=%async_computation.1 | async-start | bytes 6291456 | tf_op jit(solution)/shard_map/all_to_all | solution.py:109
  128.3 10.5 %copy-start.1 = (f32[32]{0:T(128)S(1)}, f32[32]{0:T(128)}, u32[]{:S(2)}) copy-start(f32[32]{0:T(128)} %param.15) | copy-start | bytes 388
  128.3 214.8 %all-to-all-start.2 = ((bf16[64,2,24,1536]{3,2,1,0:T(8,128)(2,1)}), bf16[64,2,24,1536]{3,2,1,0:T(8,128)(2,1)}, u32[]{:S(2)}, u32[]{:S(2)}) async-start(bf16[64,2,24,1536]{3,2,1,0:T(8,128)(2,1)} %bitcast.77), calls=%async_computation.2 | async-start | bytes 18874368 | tf_op jit(solution)/shard_map/all_to_all | solution.py:101
  365.1 11.4 %copy-start.9 = (bf16[1,128,1536]{2,1,0:T(8,128)(2,1)S(1)}, bf16[1,128,1536]{2,1,0:T(8,128)(2,1)}, u32[]{:S(2)}) copy-start(bf16[1,128,1536]{2,1,0:T(8,128)(2,1)} %param.17) | copy-start | bytes 1179652
  365.1 80.5 %all-to-all-start.3 = ((bf16[64,10,1536]{2,1,0:T(8,128)(2,1)}), bf16[64,10,1536]{2,1,0:T(8,128)(2,1)}, u32[]{:S(2)}, u32[]{:S(2)}) async-start(bf16[64,10,1536]{2,1,0:T(8,128)(2,1)} %reshape.279), calls=%async_computation.3 | async-start | bytes 6291456 | tf_op jit(solution)/shard_map/all_to_all | solution.py:120
  378.9 5.0 copy-start.8
  378.9 5.0 copy-start.13
  378.9 5.2 copy-start.11
  454.6 3.0 copy-start.10
  457.5 1.8 copy-start.5
  469.9 80.0 %all-to-all-start.4 = ((bf16[64,10,1536]{2,1,0:T(8,128)(2,1)}), bf16[64,10,1536]{2,1,0:T(8,128)(2,1)}, u32[]{:S(2)}, u32[]{:S(2)}) async-start(bf16[64,10,1536]{2,1,0:T(8,128)(2,1)} %reshape.283), calls=%async_computation.4 | async-start | bytes 6291456 | tf_op jit(solution)/shard_map/all_to_all | solution.py:110
  552.7 5.7 copy-start.3
  568.1 217.4 %all-to-all-start.6 = ((f32[1,64,24,1536]{3,2,0,1:T(8,128)}), f32[1,64,24,1536]{3,2,0,1:T(8,128)}, u32[]{:S(2)}, u32[]{:S(2)}) async-start(f32[1,64,24,1536]{3,2,0,1:T(8,128)} %convolution_bitcast_fusion), calls=%async_computation.6 | async-start | bytes 18874368 | tf_op jit(solution)/shard_map/all_to_all | solution.py:168
  578.8 335.3 %all-reduce.7.cloned.1.call-start = ((), (), s32[]{:S(2)}) async-start(), calls=%async_computation.8 | async-start | bytes 753664 | tf_op jit(solution)/shard_map/psum | solution.py:188
  580.2 424.2 %reduce-scatter.2.cloned.1.call-start = ((), (), s32[]{:S(2)}) async-start(), calls=%async_computation.9 | async-start | bytes 5898240 | tf_op jit(solution)/shard_map/reduce_scatter | solution.py:184
  800.1 1.5 copy-start.4
  815.5 13.6 %copy-start.6 = (bf16[128,4,1536]{2,1,0:T(4,128)(2,1)S(1)}, bf16[128,4,1536]{2,1,0:T(4,128)(2,1)}, u32[]{:S(2)}) copy-start(bf16[128,4,1536]{2,1,0:T(4,128)(2,1)} %copy-done.5) | copy-start | bytes 4718596
  815.5 100.4 %all-to-all-start.5 = ((bf16[64,10,1536]{2,1,0:T(8,128)(2,1)}), bf16[64,10,1536]{2,1,0:T(8,128)(2,1)}, u32[]{:S(2)}, u32[]{:S(2)}) async-start(bf16[64,10,1536]{2,1,0:T(8,128)(2,1)} %reshape.285), calls=%async_computation.5 | async-start | bytes 6291456 | tf_op jit(solution)/shard_map/all_to_all | solution.py:127
Sparse Core Ops, SparseCore 0:
  585.7 328.3 all-reduce.6
Sparse Core Ops, SparseCore 1:
  800.2 83.5 reduce-scatter.1
where the time goes:
time: 1020 us; the launch traced here: 1010 us
  waiting for transfers between devices  679 us (67%)
  local copies, waits for them, and re-layouts  104 us (10%)
  starting transfers between devices  80.5 us (8%)
  blocking collectives  75.3 us (7%)
  matrix products  33.5 us (3%)
  other arithmetic  25.9 us (3%)
  between operations  16.1 us (2%)
    all_to_all x1, waiting for transfers between devices, on_device(): lax.all_to_all(lane_grads.reshape(per_lane, ctx_count, row_share, hidden_...  205 us
    all_to_all x1, waiting for transfers between devices, on_device(): lax.all_to_all(outgoing, 'ctx', split_axis=0, concat_axis=2, tiled=True)  200 us
    psum x1, waiting for transfers between devices, on_device(): lax.psum((part_router_w, part_router_b, coef_part), ('ctx', 'rep'))  82 us
    psum x1, blocking collectives, on_device(): lax.psum((part_router_w, part_router_b, coef_part), ('ctx', 'rep'))  75.3 us
    all_to_all x1, waiting for transfers between devices, on_device(): lax.all_to_all(send_hidden, 'ctx', split_axis=0, concat_axis=0, tiled=True)  66 us
    all_to_all x1, waiting for transfers between devices, on_device(): lax.all_to_all(send_grad, 'ctx', split_axis=0, concat_axis=0, tiled=True)  64.7 us
    all_to_all x1, waiting for transfers between devices, on_device(): lax.all_to_all(out_rows.astype(jnp.bfloat16).reshape(ctx_count, capacity,...  61.5 us
  transfers between devices with their start and end apart: 9, of which 6 were waited for; matrix products, arithmetic and copies ran while one was open for 8% of the time, Pallas kernels for 0%

commit v1 on v0

v1 whole, which is shorter than its diff:
```python
import math

import jax
import jax.numpy as jnp
from jax import lax
from jax.sharding import PartitionSpec as P

PLANE = ("x", "yh", "yl")


def on_device(
    tokens, router_w, router_b, hidden, teacher_idx, merge_map, merge_coef, source_w, out_grad
):
    tok, feat = tokens.shape[1], tokens.shape[2]
    top, ffw = teacher_idx.shape[2], hidden.shape[3]
    dw = out_grad.shape[2]
    experts = router_w.shape[1]
    groups = 16
    copies = 4
    cap = 10
    slots = tok * top
    rows = 64 * cap
    quarter = ffw // 4
    grad_scale = 1.0 / math.sqrt(tok * 256)
    c, yh = lax.axis_index("c"), lax.axis_index("yh")
    x = tokens.reshape(tok, feat)
    hid = hidden.reshape(slots, ffw)
    og = out_grad.reshape(tok, dw)
    logits = jnp.dot(x, router_w, preferred_element_type=jnp.float32) + router_b
    choice = teacher_idx.reshape(tok, top)
    pick = choice[:, :, None] == jnp.arange(experts, dtype=jnp.int32)
    pick_float = pick.astype(jnp.float32)
    chosen = jnp.sum(pick_float * logits[:, None, :], axis=2)
    raised = jnp.exp(chosen)
    gate = raised / jnp.sum(raised, axis=1, keepdims=True)
    merged_id = jnp.sum(jnp.where(pick, merge_map[None, None, :], 0), axis=2)
    lane = (merged_id * copies + (jnp.arange(tok, dtype=jnp.int32) % copies)[:, None]).reshape(-1)
    onehot = (lane[:, None] == jnp.arange(64, dtype=jnp.int32)[None, :]).astype(jnp.bfloat16)
    lower = (
        jnp.arange(slots)[:, None] > jnp.arange(slots)[None, :]
    ).astype(jnp.bfloat16)
    before = jnp.dot(lower, onehot, preferred_element_type=jnp.float32)
    rank = jnp.sum(before * onehot.astype(jnp.float32), axis=1).astype(jnp.int32)
    index = jnp.where(rank < cap, lane * cap + rank, rows)
    select = (index[None, :] == jnp.arange(rows, dtype=jnp.int32)[:, None]).astype(jnp.bfloat16)
    slot_grad = (gate[:, :, None] * og[:, None, :]).astype(jnp.bfloat16).reshape(slots, dw)
    send_h = jnp.dot(select, hid, preferred_element_type=jnp.float32).astype(jnp.bfloat16)
    send_g = jnp.dot(select, slot_grad, preferred_element_type=jnp.float32).astype(jnp.bfloat16)

    ids = jnp.arange(experts, dtype=jnp.int32)
    same = merge_map[:, None] == merge_map[None, :]
    second = jnp.any(same & (ids[:, None] > ids[None, :]), axis=1)
    member = merge_map[None, :] == jnp.arange(groups, dtype=jnp.int32)[:, None]
    first_id = jnp.sum(jnp.where(member & ~second[None, :], ids[None, :], 0), axis=1)
    second_id = jnp.sum(jnp.where(member & second[None, :], ids[None, :], 0), axis=1)
    mine = lax.dynamic_slice_in_dim(source_w, (c * 2 + yh) * quarter, quarter, 2)
    merged = (
        merge_coef[first_id][:, None, None] * mine[first_id].astype(jnp.float32)
        + merge_coef[second_id][:, None, None] * mine[second_id].astype(jnp.float32)
    ).astype(jnp.bfloat16)
    share = source_w.shape[1]

    part = lax.all_to_all(merged, PLANE, 0, 0, tiled=True)
    full = lax.all_gather(part, ("z", "c"))
    weight = (
        full.reshape(8, 2, 4, 2, 2, share, quarter)
        .transpose(2, 4, 0, 5, 1, 3, 6)
        .reshape(dw, ffw)
    )
    got_h = lax.all_to_all(send_h.reshape(groups, -1, ffw), PLANE, 0, 0, tiled=True)
    got_g = lax.all_to_all(send_g.reshape(groups, -1, dw), PLANE, 0, 0, tiled=True)
    got_h = got_h.reshape(rows, ffw)
    got_g = got_g.reshape(rows, dw)
    out_rows = lax.dot_general(
        got_h, weight, (((1,), (1,)), ((), ())), preferred_element_type=jnp.float32
    ).astype(jnp.bfloat16)
    back_rows = jnp.dot(got_g, weight, preferred_element_type=jnp.float32).astype(jnp.bfloat16)
    lane_grad = lax.dot_general(
        got_g, got_h, (((0,), (0,)), ((), ())), preferred_element_type=jnp.float32
    )
    home_out = lax.all_to_all(out_rows.reshape(groups, -1, dw), PLANE, 0, 0, tiled=True)
    home_back = lax.all_to_all(back_rows.reshape(groups, -1, ffw), PLANE, 0, 0, tiled=True)
    home_out = home_out.reshape(rows, dw)
    home_back = home_back.reshape(rows, ffw)
    pieces = (
        lane_grad.reshape(4, 2, 8, share, 2, 2, quarter)
        .transpose(2, 5, 0, 4, 1, 3, 6)
        .reshape(16, 16 * share, quarter)
    )
    summed = lax.psum_scatter(pieces, ("z", "c"), scatter_dimension=0, tiled=False)
    merged_grad = lax.all_to_all(
        summed.reshape(groups, share, quarter), PLANE, 0, 0, tiled=True
    )

    spread = (
        index[:, None] == jnp.arange(rows, dtype=jnp.int32)[None, :]
    ).astype(jnp.bfloat16)
    slot_out = jnp.dot(spread, home_out, preferred_element_type=jnp.float32)
    slot_out = slot_out.reshape(tok, top, dw)
    hidden_grad = (
        jnp.dot(spread, home_back, preferred_element_type=jnp.float32)
        .astype(jnp.bfloat16)
        .reshape(1, tok, top, ffw)
    )
    mixed = jnp.sum(gate[:, :, None] * slot_out, axis=1).astype(jnp.bfloat16)
    score = jnp.sum(og[:, None, :].astype(jnp.float32) * slot_out, axis=2)
    chosen_grad = gate * (score - jnp.sum(gate * score, axis=1, keepdims=True))
    logit_grad = jnp.sum(pick_float * chosen_grad[:, :, None], axis=1)
    logit_half = logit_grad.astype(jnp.bfloat16)
    token_grad = lax.dot_general(
        logit_half, router_w, (((1,), (1,)), ((), ())), preferred_element_type=jnp.float32
    ).astype(jnp.bfloat16)
    part_w = lax.dot_general(
        x, logit_half, (((0,), (0,)), ((), ())), preferred_element_type=jnp.float32
    )
    part_b = jnp.sum(logit_grad, axis=0)
    source_grad = merged_grad[merge_map]
    mine_out = lax.dynamic_slice_in_dim(source_w, (yh * 2 + c) * quarter, quarter, 2)
    part_c = jnp.sum(source_grad * mine_out.astype(jnp.float32), axis=(1, 2))
    source_w_grad = source_grad * (merge_coef * grad_scale)[:, None, None]
    every = ("x", "yl", "z", "yh", "c")
    sum_w, sum_b, sum_c = lax.psum((part_w, part_b, part_c), every)
    return (
        mixed.reshape(1, tok, dw),
        hidden_grad,
        token_grad.reshape(1, tok, feat),
        sum_w * grad_scale,
        sum_b * grad_scale,
        sum_c * grad_scale,
        source_w_grad,
    )


def solution(mesh):
    fine = jax.sharding.Mesh(mesh.devices.reshape(4, 2, 8, 2, 2), ("x", "yl", "z", "yh", "c"))
    ctx, rep = ("x", "yl", "z"), ("yh", "c")
    in_specs = (
        P(rep, ctx, None),
        P(),
        P(),
        P(rep, ctx, None, None),
        P(rep, ctx, None),
        P(),
        P(),
        P(None, ctx, None),
        P(rep, ctx, None),
    )
    out_specs = (
        P(rep, ctx, None),
        P(rep, ctx, None, None),
        P(rep, ctx, None),
        P(),
        P(),
        P(),
        P(None, ctx, rep),
    )
    return jax.shard_map(
        on_device, mesh=fine, in_specs=in_specs, out_specs=out_specs, check_vma=False
    )
```

time: 1020 us -> 538 us (0.53)
  waiting for transfers between devices: 679 us -> 305 us
  local copies, waits for them, and re-layouts: 104 us -> 52.3 us
  starting transfers between devices: 80.5 us -> 28.8 us
  other arithmetic: 25.9 us -> 7.55 us
  blocking collectives: 75.3 us -> 90.6 us
    all_to_all x7 -> x5, waiting for transfers between devices: 597 us -> 70.3 us  [the longest x1 21.3 us: on_device(): lax.all_to_all(send_h.reshape(groups, -1, ffw), PLANE, 0, 0, tiled=True)]
    psum x1, waiting for transfers between devices: 82 us -> 235 us  [on_device(): sum_w, sum_b, sum_c = lax.psum((part_w, part_b, part_c), every)]
    all_to_all x7 -> x5, starting transfers between devices: 80.4 us -> 28.7 us  [the longest x1 7.5 us: on_device(): lax.all_to_all(back_rows.reshape(groups, -1, ffw), PLANE, 0, 0, tiled=True)]
    gather x7 -> x4, local copies, waits for them, and re-layouts: 18.9 us -> 2.55 us  [the longest x1 0.67 us: on_device(): merge_coef[first_id][:, None, None] * mine[first_id].astype(jnp.float32)]
    all_to_all x0 -> x1, blocking collectives: none -> 15.1 us  [on_device(): part = lax.all_to_all(merged, PLANE, 0, 0, tiled=True)]
    reshape x13 -> x6, local copies, waits for them, and re-layouts: 43.6 us -> 33.9 us  [the longest x1 11.2 us: on_device(): weight = full.reshape(8, 2, 4, 2, 2, share, quarter).transpose(2, 4, 0, 5...]
    dot_general x6 -> x10, matrix products: 32.2 us -> 37.2 us  [the longest x1 7.51 us: on_device(): lax.dot_general(got_h, weight, (((1,), (1,)), ((), ())), preferred_elemen...]
  transfers between devices with their start and end apart: 9 -> 8, of which waited for: 6 -> 5; matrix products, arithmetic and copies ran while one was open for 8% -> 16% of each run, Pallas kernels for 0% -> 0%
where the time goes in v1:
time: 538 us; the launch traced here: 537 us
  waiting for transfers between devices  305 us (57%)
  blocking collectives  90.6 us (17%)
  local copies, waits for them, and re-layouts  52.3 us (10%)
  matrix products  38.5 us (7%)
  starting transfers between devices  28.8 us (5%)
  between operations  14 us (3%)
  other arithmetic  7.55 us (1%)
    psum x1, waiting for transfers between devices, on_device(): sum_w, sum_b, sum_c = lax.psum((part_w, part_b, part_c), every)  235 us
    psum x1, blocking collectives, on_device(): sum_w, sum_b, sum_c = lax.psum((part_w, part_b, part_c), every)  75.6 us
    all_to_all x1, waiting for transfers between devices, on_device(): lax.all_to_all(send_h.reshape(groups, -1, ffw), PLANE, 0, 0, tiled=True)  21.3 us
    all_to_all x1, waiting for transfers between devices, on_device(): lax.all_to_all(back_rows.reshape(groups, -1, ffw), PLANE, 0, 0, tiled=True)  18.4 us
    all_to_all x1, waiting for transfers between devices, on_device(): lax.all_to_all(send_g.reshape(groups, -1, dw), PLANE, 0, 0, tiled=True)  16.8 us
    all_to_all x1, blocking collectives, on_device(): part = lax.all_to_all(merged, PLANE, 0, 0, tiled=True)  15.1 us
    all_to_all x1, waiting for transfers between devices, on_device(): lax.all_to_all(out_rows.reshape(groups, -1, dw), PLANE, 0, 0, tiled=True)  13.8 us
    reshape x1, local copies, waits for them, and re-layouts, on_device(): weight = full.reshape(8, 2, 4, 2, 2, share, quarter).transpose(2, 4, 0, 5...  11.2 us
  transfers between devices with their start and end apart: 8, of which 5 were waited for; matrix products, arithmetic and copies ran while one was open for 16% of the time, Pallas kernels for 0%

profile of v1, /device:TPU:1, one launch (start us, length us, event | category | flops | bytes accessed | tf_op | source)
XLA Modules:
  0.0 537.0 jit_solution(14346176282419523803)
XLA Ops:
  7.2 0.9 fusion.15
  8.2 0.8 select_reduce_fusion.5
  9.0 1.1 constant_dynamic-slice_fusion
  10.2 0.6 gather_fusion.3
  10.8 0.6 gather_fusion.1
  11.4 0.7 gather_fusion.2
  12.1 0.7 gather_fusion
  12.7 0.2 add_convert_fusion
  12.9 15.1 %all_to_all.30 = bf16[16,24,384]{2,1,0:T(8,128)(2,1)} all-to-all(bf16[16,24,384]{2,1,0:T(8,128)(2,1)S(1)} %add_convert_fusion), channel_id=1, replica_groups=mesh['x'=4,'yl'=2,'z'=8,'yh'=2,'c'=2] {'x','yh','yl'}, dimensions={0} | all-to-all | bytes 589824 | tf_op jit(solution)/shard_map/all_to_all | solution.py:63
  28.5 2.2 mul.163.clone
  30.7 4.9 mul.164
  35.6 0.2 convolution_add_fusion
  36.2 0.3 fusion.5
  36.5 4.5 convolution_convert_fusion.3
  40.9 3.8 all-to-all-start.3
  44.7 3.7 reshape.265
  48.4 3.9 convolution_convert_fusion.4
  52.4 16.8 %all-to-all-done.3 = bf16[16,40,1536]{2,1,0:T(8,128)(2,1)S(1)} async-done(((bf16[16,40,1536]{2,1,0:T(8,128)(2,1)}), bf16[16,40,1536]{2,1,0:T(8,128)(2,1)S(1)}, u32[]{:S(2)}, u32[]{:S(2)}) %all-to-all-start.3) | async-done | bytes 1966112 | tf_op jit(solution)/shard_map/all_to_all | solution.py:71
  69.2 5.4 %all-to-all-start = ((bf16[16,40,1536]{2,1,0:T(8,128)(2,1)}), bf16[16,40,1536]{2,1,0:T(8,128)(2,1)}, u32[]{:S(2)}, u32[]{:S(2)}) async-start(bf16[16,40,1536]{2,1,0:T(8,128)(2,1)} %bitcast.82), calls=%async_computation | async-start | bytes 3932160 | tf_op jit(solution)/shard_map/all_to_all | solution.py:70
  74.6 2.5 copy.46
  77.1 21.3 %all-to-all-done = bf16[16,40,1536]{2,1,0:T(8,128)(2,1)} async-done(((bf16[16,40,1536]{2,1,0:T(8,128)(2,1)}), bf16[16,40,1536]{2,1,0:T(8,128)(2,1)}, u32[]{:S(2)}, u32[]{:S(2)}) %all-to-all-start) | async-done | bytes 1966112 | tf_op jit(solution)/shard_map/all_to_all | solution.py:70
  98.4 4.0 copy.47
  102.4 6.1 %convolution_bitcast_fusion = f32[8,2,4,2,2,24,384]{6,5,1,3,0,4,2:T(8,128)S(1)} fusion(bf16[4,2,8,24,640,1,1]{4,3,6,5,2,1,0:T(8,128)(2,1)} %bitcast.84, bf16[2,2,384,640,1,1,1]{3,2,1,0,6,5,4:T(8,128)(2,1)} %bitcast.85), kind=kOutput, calls=%fused_computation.8 | convolution fusion | flops 3019898880 | bytes 13369344 | tf_op jit(solution)/shard_map/dot_general | solution.py:78
  108.5 4.8 copy.48
  113.3 8.6 %copy.53 = bf16[8,2,4,2,2,24,384]{6,3,1,5,0,4,2:T(2,128)(2,1)} copy(bf16[8,2,4,2,2,24,384]{6,5,4,3,2,1,0:T(8,128)(2,1)} %bitcast.78) | data formatting | bytes 9437184 | tf_op jit(solution)/shard_map/reshape | solution.py:66
  121.9 11.2 %reshape.269 = bf16[1536,1536]{1,0:T(8,128)(2,1)} reshape(bf16[4,2,8,24,2,2,384]{6,5,4,3,2,1,0:T(2,128)(2,1)} %bitcast.75) | data formatting | bytes 9437184 | tf_op jit(solution)/shard_map/reshape | solution.py:68
  133.1 7.5 %convolution_convert_fusion.2 = bf16[640,1536]{1,0:T(8,128)(2,1)} fusion(bf16[640,1536]{1,0:T(8,128)(2,1)} %bitcast.4, bf16[1536,1536]{1,0:T(8,128)(2,1)} %reshape.269), kind=kOutput, calls=%fused_computation.11 | convolution fusion | flops 3020881920 | bytes 8650752 | tf_op jit(solution)/shard_map/dot_general | solution.py:74
  140.7 5.4 %all-to-all-start.2 = ((bf16[16,40,1536]{2,1,0:T(8,128)(2,1)}), bf16[16,40,1536]{2,1,0:T(8,128)(2,1)}, u32[]{:S(2)}, u32[]{:S(2)}) async-start(bf16[16,40,1536]{2,1,0:T(8,128)(2,1)} %bitcast.81), calls=%async_computation.2 | async-start | bytes 3932160 | tf_op jit(solution)/shard_map/all_to_all | solution.py:81
  146.1 0.7 convert_element_type.90
  146.8 0.9 copy.41
  147.7 6.8 %convolution_convert_fusion.1 = bf16[640,1536]{1,0:T(8,128)(2,1)} fusion(bf16[640,1536]{1,0:T(8,128)(2,1)S(1)} %bitcast.77, bf16[1536,1536]{1,0:T(8,128)(2,1)} %reshape.269), kind=kOutput, calls=%fused_computation.10 | convolution fusion | flops 3020881920 | bytes 8650752 | tf_op jit(solution)/shard_map/dot_general | solution.py:77
  154.5 13.8 %all-to-all-done.2 = bf16[16,40,1536]{2,1,0:T(8,128)(2,1)} async-done(((bf16[16,40,1536]{2,1,0:T(8,128)(2,1)}), bf16[16,40,1536]{2,1,0:T(8,128)(2,1)}, u32[]{:S(2)}, u32[]{:S(2)}) %all-to-all-start.2) | async-done | bytes 1966112 | tf_op jit(solution)/shard_map/all_to_all | solution.py:81
  168.3 7.5 %all-to-all-start.4 = ((bf16[16,40,1536]{2,1,0:T(8,128)(2,1)}), bf16[16,40,1536]{2,1,0:T(8,128)(2,1)S(1)}, u32[]{:S(2)}, u32[]{:S(2)}) async-start(bf16[16,40,1536]{2,1,0:T(8,128)(2,1)} %bitcast.79), calls=%async_computation.4 | async-start | bytes 3932160 | tf_op jit(solution)/shard_map/all_to_all | solution.py:82
  175.9 4.1 multiply_reduce_fusion
  180.1 0.1 select_reduce_fusion
  180.2 1.1 convolution_bitcast_fusion.1
  181.3 18.4 %all-to-all-done.4 = bf16[16,40,1536]{2,1,0:T(8,128)(2,1)S(1)} async-done(((bf16[16,40,1536]{2,1,0:T(8,128)(2,1)}), bf16[16,40,1536]{2,1,0:T(8,128)(2,1)S(1)}, u32[]{:S(2)}, u32[]{:S(2)}) %all-to-all-start.4) | async-done | bytes 1966112 | tf_op jit(solution)/shard_map/all_to_all | solution.py:82
  199.8 2.6 convolution_convert_fusion.5
  202.4 3.9 reshape.276
  206.3 1.3 fusion
  207.6 6.7 %all-to-all-start.5 = ((f32[16,24,384]{2,1,0:T(8,128)}), f32[16,24,384]{2,1,0:T(8,128)S(1)}, u32[]{:S(2)}, u32[]{:S(2)}) async-start(f32[16,24,384]{2,1,0:T(8,128)} %bitcast.86), calls=%async_computation.6 | async-start | bytes 1179648 | tf_op jit(solution)/shard_map/all_to_all | solution.py:91
  214.3 234.8 %all-reduce.3.cloned.1.call-done = f32[2880,32]{0,1:T(8,128)} async-done(((f32[2880,32]{0,1:T(8,128)}), f32[2880,32]{0,1:T(8,128)}) %all-reduce.3.cloned.1.call-update) | async-done | bytes 368656 | tf_op jit(solution)/shard_map/psum | solution.py:122
  449.0 1.8 broadcast_multiply_fusion.1
  450.8 0.6 gather_fusion.4
  451.4 2.4 broadcast_multiply_fusion
  453.9 75.6 %all-reduce = (f32[32]{0:T(128)S(1)}, f32[32]{0:T(128)S(1)}) all-reduce(f32[32]{0:T(128)S(1)} %get-tuple-element.9, f32[32]{0:T(128)S(1)} %get-tuple-element.16), channel_id=1, replica_groups=mesh['x'=4,'yl'=2,'z'=8,'yh'=2,'c'=2] {'x','yl','z','yh','c'}, use_global_device_ids=true, to_apply=%region_13.14 | all-reduce | flops 64 | bytes 512 | tf_op jit(solution)/shard_map/psum | solution.py:122
  529.4 0.5 broadcast_multiply_fusion.4
  529.9 0.5 broadcast_multiply_fusion.3
  (48 shorter events, 1.0 us)
Async XLA Ops:
  7.2 28.4 %copy-start = (bf16[1,128,2880]{1,2,0:T(8,128)(2,1)S(1)}, bf16[1,128,2880]{1,2,0:T(8,128)(2,1)}, u32[]{:S(2)}) copy-start(bf16[1,128,2880]{1,2,0:T(8,128)(2,1)} %param.9) | copy-start | bytes 2211844
  7.2 4.2 copy-start.1
  7.2 106.1 %all-gather.3.cloned.1.call-start = ((), (), s32[]{:S(2)}) async-start(), calls=%async_computation.9 | async-start | bytes 5013504 | tf_op jit(solution)/shard_map/all_gather | solution.py:64
  10.1 17.9 %copy-start.5 = (s32[1,128,4]{1,2,0:T(4,128)S(1)}, s32[1,128,4]{1,2,0:T(4,128)}, u32[]{:S(2)}) copy-start(s32[1,128,4]{1,2,0:T(4,128)} %param.13) | copy-start | bytes 6148
  10.1 17.9 %copy-start.6 = (s32[32]{0:T(128)S(1)}, s32[32]{0:T(128)}, u32[]{:S(2)}) copy-start(s32[32]{0:T(128)} %param.14) | copy-start | bytes 388
  10.1 18.2 %copy-start.4 = (bf16[1,128,1536]{2,1,0:T(8,128)(2,1)S(1)}, bf16[1,128,1536]{2,1,0:T(8,128)(2,1)}, u32[]{:S(2)}) copy-start(bf16[1,128,1536]{2,1,0:T(8,128)(2,1)} %param.17) | copy-start | bytes 1179652
  30.7 4.9 copy-start.2
  30.7 4.9 copy-start.7
  40.9 28.2 %all-to-all-start.3 = ((bf16[16,40,1536]{2,1,0:T(8,128)(2,1)}), bf16[16,40,1536]{2,1,0:T(8,128)(2,1)S(1)}, u32[]{:S(2)}, u32[]{:S(2)}) async-start(bf16[16,40,1536]{2,1,0:T(8,128)(2,1)} %bitcast.83), calls=%async_computation.3 | async-start | bytes 3932160 | tf_op jit(solution)/shard_map/all_to_all | solution.py:71
  69.2 29.2 %all-to-all-start = ((bf16[16,40,1536]{2,1,0:T(8,128)(2,1)}), bf16[16,40,1536]{2,1,0:T(8,128)(2,1)}, u32[]{:S(2)}, u32[]{:S(2)}) async-start(bf16[16,40,1536]{2,1,0:T(8,128)(2,1)} %bitcast.82), calls=%async_computation | async-start | bytes 3932160 | tf_op jit(solution)/shard_map/all_to_all | solution.py:70
  74.5 133.0 %reduce-scatter.2.cloned.1.call-start = ((), (), s32[]{:S(2)}) async-start(), calls=%async_computation.8 | async-start | bytes 10027008 | tf_op jit(solution)/shard_map/reduce_scatter | solution.py:90
  140.7 27.7 %all-to-all-start.2 = ((bf16[16,40,1536]{2,1,0:T(8,128)(2,1)}), bf16[16,40,1536]{2,1,0:T(8,128)(2,1)}, u32[]{:S(2)}, u32[]{:S(2)}) async-start(bf16[16,40,1536]{2,1,0:T(8,128)(2,1)} %bitcast.81), calls=%async_computation.2 | async-start | bytes 3932160 | tf_op jit(solution)/shard_map/all_to_all | solution.py:81
  168.3 31.4 %all-to-all-start.4 = ((bf16[16,40,1536]{2,1,0:T(8,128)(2,1)}), bf16[16,40,1536]{2,1,0:T(8,128)(2,1)S(1)}, u32[]{:S(2)}, u32[]{:S(2)}) async-start(bf16[16,40,1536]{2,1,0:T(8,128)(2,1)} %bitcast.79), calls=%async_computation.4 | async-start | bytes 3932160 | tf_op jit(solution)/shard_map/all_to_all | solution.py:82
  175.8 273.2 %all-reduce.3.cloned.1.call-start = ((), (), s32[]{:S(2)}) async-start(), calls=%async_computation.7 | async-start | bytes 753664 | tf_op jit(solution)/shard_map/psum | solution.py:122
  202.4 3.9 copy-start.3
  207.6 243.2 %all-to-all-start.5 = ((f32[16,24,384]{2,1,0:T(8,128)}), f32[16,24,384]{2,1,0:T(8,128)S(1)}, u32[]{:S(2)}, u32[]{:S(2)}) async-start(f32[16,24,384]{2,1,0:T(8,128)} %bitcast.86), calls=%async_computation.6 | async-start | bytes 1179648 | tf_op jit(solution)/shard_map/all_to_all | solution.py:91
Sparse Core Ops, SparseCore 0:
  28.1 43.7 all-gather.2
  113.4 76.8 reduce-scatter.1
  196.4 252.6 all-reduce.2

commit v2 on v1

--- a/solution.py
+++ b/solution.py
@@ -3,9 +3,303 @@
 import jax
 import jax.numpy as jnp
 from jax import lax
+from jax.experimental import pallas as pl
+from jax.experimental.pallas import tpu as pltpu
 from jax.sharding import PartitionSpec as P
 
-PLANE = ("x", "yh", "yl")
+MESH = pl.DeviceIdType.MESH
+BF = jnp.bfloat16
+F32 = jnp.float32
+
+
+def offset(k, x, y):
+    px = lax.rem(x + k // 4, 4)
+    py = lax.rem(y + lax.rem(k, 4), 4)
+    return px, py
+
+
+def plane_id(px, py):
+    return {"x": px, "yl": lax.rem(py, 2), "yh": py // 2}
+
+
+def remote(src, dst, send, recv, where):
+    return pltpu.make_async_remote_copy(
+        src_ref=src, dst_ref=dst, send_sem=send, recv_sem=recv, device_id=where,
+        device_id_type=MESH,
+    )
+
+
+def core_kernel(
+    wq, send_h, send_g, home_out, home_back, grad_out,
+    weight, recv_h, recv_g, mat_h, mat_g, mat_w, out_send, back_send,
+    part, sib, ring_send, ring_recv, last,
+    a_s, a_r, h_s, h_r, g_s, g_r, zp_s, zp_r, zm_s, zm_r, w_s, w_r,
+    o_s, o_r, b_s, b_r, e_s, e_r, rp_s, rp_r, rm_s, rm_r, l_s, l_r,
+):
+    x, yl, z = lax.axis_index("x"), lax.axis_index("yl"), lax.axis_index("z")
+    yh, c = lax.axis_index("yh"), lax.axis_index("c")
+    y = yh * 2 + yl
+    me = x * 4 + y
+    xy = x * 2 + yl
+    up, down = lax.rem(z + 1, 8), lax.rem(z + 7, 8)
+    sibling = {"c": 1 - c}
+
+    barrier = pltpu.get_barrier_semaphore()
+
+    def greet(k, carry):
+        px, py = offset(k, x, y)
+        pl.semaphore_signal(barrier, inc=1, device_id=plane_id(px, py), device_id_type=MESH)
+        return carry
+
+    lax.fori_loop(1, 16, greet, 0)
+    for where in ({"z": up}, {"z": down}, sibling):
+        pl.semaphore_signal(barrier, inc=1, device_id=where, device_id_type=MESH)
+    pl.semaphore_wait(barrier, 18)
+
+    quarter = pl.ds(pl.multiple_of((c * 2 + yh) * 384, 384), 384)
+    half = pl.ds(pl.multiple_of(c * 768, 768), 768)
+
+    def a_copy(k):
+        px, py = offset(k, x, y)
+        return remote(
+            wq.at[px * 4 + py], weight.at[xy, z, :, :, quarter], a_s.at[k], a_r.at[k],
+            plane_id(px, py),
+        )
+
+    def h_copy(k):
+        px, py = offset(k, x, y)
+        return remote(
+            send_h.at[pl.ds(5 * (px * 4 + py), 5)], recv_h.at[pl.ds(5 * me, 5)],
+            h_s.at[k], h_r.at[k], plane_id(px, py),
+        )
+
+    def g_copy(k):
+        px, py = offset(k, x, y)
+        return remote(
+            send_g.at[pl.ds(5 * (px * 4 + py), 5)], recv_g.at[pl.ds(5 * me, 5)],
+            g_s.at[k], g_r.at[k], plane_id(px, py),
+        )
+
+    def o_copy(k):
+        px, py = offset(k, x, y)
+        return remote(
+            out_send.at[pl.ds(5 * (px * 4 + py), 5)], home_out.at[pl.ds(5 * me, 5)],
+            o_s.at[k], o_r.at[k], plane_id(px, py),
+        )
+
+    def b_copy(k):
+        px, py = offset(k, x, y)
+        return remote(
+            back_send.at[pl.ds(5 * (px * 4 + py), 5)], home_back.at[pl.ds(5 * me, 5)],
+            b_s.at[k], b_r.at[k], plane_id(px, py),
+        )
+
+    def l_copy(k):
+        px, py = offset(k, x, y)
+        return remote(
+            last.at[py // 2, px * 2 + lax.rem(py, 2)], grad_out.at[me],
+            l_s.at[k], l_r.at[k], plane_id(px, py),
+        )
+
+    def each(do):
+        def step(k, carry):
+            do(k)
+            return carry
+
+        lax.fori_loop(1, 16, step, 0)
+
+    each(lambda k: a_copy(k).start())
+    each(lambda k: h_copy(k).start())
+    each(lambda k: g_copy(k).start())
+    own = pl.ds(5 * me, 5)
+    weight[xy, z, :, :, quarter] = wq[me]
+    recv_h[own] = send_h[own]
+    recv_g[own] = send_g[own]
+    each(lambda k: a_copy(k).wait_recv())
+
+    def block(b):
+        return weight.at[:, b, :, :, half]
+
+    def w_copy(i):
+        b = lax.rem(z + 8 - i, 8) if i <= 4 else lax.rem(z + i - 4, 8)
+        return remote(block(b), block(b), w_s.at[i], w_r.at[i], sibling)
+
+    def zp_copy(s):
+        b = lax.rem(z + 8 - s, 8)
+        return remote(block(b), block(b), zp_s.at[s], zp_r.at[s], {"z": up})
+
+    def zm_copy(s):
+        b = lax.rem(z + s, 8)
+        return remote(block(b), block(b), zm_s.at[s], zm_r.at[s], {"z": down})
+
+    zp_copy(0).start()
+    zm_copy(0).start()
+    w_copy(0).start()
+    for s in range(4):
+        zp_copy(s).wait_recv()
+        if s < 3:
+            zp_copy(s + 1).start()
+        w_copy(s + 1).start()
+        if s < 3:
+            zm_copy(s).wait_recv()
+            if s < 2:
+                zm_copy(s + 1).start()
+            w_copy(s + 5).start()
+
+    each(lambda k: h_copy(k).wait_recv())
+
+    def shape_h(i, carry):
+        mat_h[pl.ds(pl.multiple_of(i * 80, 80), 80), :] = (
+            recv_h[pl.ds(i * 10, 10)].astype(F32).reshape(80, 1536).astype(BF)
+        )
+        return carry
+
+    lax.fori_loop(0, 8, shape_h, 0)
+    each(lambda k: g_copy(k).wait_recv())
+
+    def shape_g(i, carry):
+        mat_g[pl.ds(pl.multiple_of(i * 80, 80), 80), :] = (
+            recv_g[pl.ds(i * 10, 10)].astype(F32).reshape(80, 1536).astype(BF)
+        )
+        return carry
+
+    lax.fori_loop(0, 8, shape_g, 0)
+
+    def outer(i, carry):
+        cols = pl.ds(pl.multiple_of(i * 384, 384), 384)
+        tile = lax.dot_general(
+            mat_g[:, cols], mat_h[...], (((0,), (0,)), ((), ())), preferred_element_type=F32
+        )
+        part[pl.ds(i * 2, 2)] = tile.reshape(2, 8, 3, 8, 1536).astype(BF)
+        return carry
+
+    lax.fori_loop(0, 4, outer, 0)
+
+    def e_copy(h):
+        there = pl.ds(pl.multiple_of(h * 768 + (1 - c) * 384, 384), 384)
+        return remote(
+            part.at[:, :, :, :, there], sib.at[h], e_s.at[h], e_r.at[h], sibling
+        )
+
+    for h in range(2):
+        e_copy(h).start()
+    for i in range(8):
+        w_copy(i).wait_recv()
+
+    def shape_w(i, carry):
+        mat_w[pl.ds(pl.multiple_of(i * 192, 192), 192), :] = (
+            weight[i].astype(F32).reshape(192, 1536).astype(BF)
+        )
+        return carry
+
+    lax.fori_loop(0, 8, shape_w, 0)
+
+    def forward(j, carry):
+        span = pl.ds(pl.multiple_of(j * 256, 256), 256)
+        tile = lax.dot_general(
+            mat_h[...], mat_w[span, :], (((1,), (1,)), ((), ())), preferred_element_type=F32
+        )
+        out_send[:, :, span] = tile.reshape(80, 8, 256).astype(BF)
+        return carry
+
+    lax.fori_loop(0, 6, forward, 0)
+    each(lambda k: o_copy(k).start())
+    home_out[own] = out_send[own]
+
+    def backward(j, carry):
+        span = pl.ds(pl.multiple_of(j * 256, 256), 256)
+        tile = jnp.dot(mat_g[...], mat_w[:, span], preferred_element_type=F32)
+        back_send[:, :, span] = tile.reshape(80, 8, 256).astype(BF)
+        return carry
+
+    lax.fori_loop(0, 6, backward, 0)
+    each(lambda k: b_copy(k).start())
+    home_back[own] = back_send[own]
+
+    for h in range(2):
+        e_copy(h).wait_recv()
+
+    def local(h, b):
+        here = pl.ds(pl.multiple_of(h * 768 + c * 384, 384), 384)
+        return part[:, b, :, :, here].astype(F32) + sib[h, :, b].astype(F32)
+
+    def ring(h, s):
+        if h == 0:
+            return remote(
+                ring_send.at[0, s], ring_recv.at[0, s], rp_s.at[s], rp_r.at[s], {"z": up}
+            )
+        return remote(
+            ring_send.at[1, s], ring_recv.at[1, s], rm_s.at[s], rm_r.at[s], {"z": down}
+        )
+
+    for s in range(7):
+        for h in range(2):
+            b = lax.rem(z + 15 - s, 8) if h == 0 else lax.rem(z + 1 + s, 8)
+            total = local(h, b)
+            if s > 0:
+                ring(h, s - 1).wait_recv()
+                total = total + ring_recv[h, s - 1].astype(F32)
+            ring_send[h, s] = total.astype(BF)
+            ring(h, s).start()
+    for h in range(2):
+        total = local(h, z)
+        ring(h, 6).wait_recv()
+        last[h] = total + ring_recv[h, 6].astype(F32)
+    each(lambda k: l_copy(k).start())
+    grad_out[me] = last[yh, xy]
+
+    each(lambda k: a_copy(k).wait_send())
+    each(lambda k: h_copy(k).wait_send())
+    each(lambda k: g_copy(k).wait_send())
+    for s in range(4):
+        zp_copy(s).wait_send()
+    for s in range(3):
+        zm_copy(s).wait_send()
+    for i in range(8):
+        w_copy(i).wait_send()
+    for h in range(2):
+        e_copy(h).wait_send()
+        for s in range(7):
+            ring(h, s).wait_send()
+    each(lambda k: o_copy(k).wait())
+    each(lambda k: b_copy(k).wait())
+    each(lambda k: l_copy(k).wait())
+
+
+def exchange(wq, send_h, send_g):
+    vmem = pl.BlockSpec(memory_space=pltpu.VMEM)
+    dma = lambda n: pltpu.SemaphoreType.DMA((n,))
+    rows = pltpu.VMEM((80, 8, 1536), BF)
+    mat = pltpu.VMEM((640, 1536), BF)
+    return pl.pallas_call(
+        core_kernel,
+        out_shape=(
+            jax.ShapeDtypeStruct((80, 8, 1536), BF),
+            jax.ShapeDtypeStruct((80, 8, 1536), BF),
+            jax.ShapeDtypeStruct((16, 3, 8, 384), F32),
+        ),
+        in_specs=[vmem] * 3,
+        out_specs=(vmem,) * 3,
+        scratch_shapes=[
+            pltpu.VMEM((8, 8, 3, 8, 1536), BF),
+            rows, rows, mat, mat,
+            pltpu.VMEM((1536, 1536), BF),
+            rows, rows,
+            pltpu.VMEM((8, 8, 3, 8, 1536), BF),
+            pltpu.VMEM((2, 8, 8, 3, 8, 384), BF),
+            pltpu.VMEM((2, 7, 8, 3, 8, 384), BF),
+            pltpu.VMEM((2, 7, 8, 3, 8, 384), BF),
+            pltpu.VMEM((2, 8, 3, 8, 384), F32),
+            dma(16), dma(16), dma(16), dma(16), dma(16), dma(16),
+            dma(4), dma(4), dma(3), dma(3), dma(8), dma(8),
+            dma(16), dma(16), dma(16), dma(16), dma(2), dma(2),
+            dma(7), dma(7), dma(7), dma(7), dma(16), dma(16),
+        ],
+        compiler_params=pltpu.CompilerParams(
+            collective_id=0, has_side_effects=True, vmem_limit_bytes=64000000
+        ),
+        name="exchange",
+    )(wq, send_h, send_g)
 
 
 def on_device(
@@ -60,37 +354,14 @@
     ).astype(jnp.bfloat16)
     share = source_w.shape[1]
 
-    part = lax.all_to_all(merged, PLANE, 0, 0, tiled=True)
-    full = lax.all_gather(part, ("z", "c"))
-    weight = (
-        full.reshape(8, 2, 4, 2, 2, share, quarter)
-        .transpose(2, 4, 0, 5, 1, 3, 6)
-        .reshape(dw, ffw)
-    )
-    got_h = lax.all_to_all(send_h.reshape(groups, -1, ffw), PLANE, 0, 0, tiled=True)
-    got_g = lax.all_to_all(send_g.reshape(groups, -1, dw), PLANE, 0, 0, tiled=True)
-    got_h = got_h.reshape(rows, ffw)
-    got_g = got_g.reshape(rows, dw)
-    out_rows = lax.dot_general(
-        got_h, weight, (((1,), (1,)), ((), ())), preferred_element_type=jnp.float32
-    ).astype(jnp.bfloat16)
-    back_rows = jnp.dot(got_g, weight, preferred_element_type=jnp.float32).astype(jnp.bfloat16)
-    lane_grad = lax.dot_general(
-        got_g, got_h, (((0,), (0,)), ((), ())), preferred_element_type=jnp.float32
-    )
-    home_out = lax.all_to_all(out_rows.reshape(groups, -1, dw), PLANE, 0, 0, tiled=True)
-    home_back = lax.all_to_all(back_rows.reshape(groups, -1, ffw), PLANE, 0, 0, tiled=True)
+    home_out, home_back, merged_grad = exchange(
+        merged.reshape(groups, 3, 8, quarter),
+        send_h.reshape(80, 8, ffw),
+        send_g.reshape(80, 8, dw),
+    )
     home_out = home_out.reshape(rows, dw)
     home_back = home_back.reshape(rows, ffw)
-    pieces = (
-        lane_grad.reshape(4, 2, 8, share, 2, 2, quarter)
-        .transpose(2, 5, 0, 4, 1, 3, 6)
-        .reshape(16, 16 * share, quarter)
-    )
-    summed = lax.psum_scatter(pieces, ("z", "c"), scatter_dimension=0, tiled=False)
-    merged_grad = lax.all_to_all(
-        summed.reshape(groups, share, quarter), PLANE, 0, 0, tiled=True
-    )
+    merged_grad = merged_grad.reshape(groups, share, quarter)
 
     spread = (
         index[:, None] == jnp.arange(rows, dtype=jnp.int32)[None, :]

time: 538 us -> 435 us (0.81)
  waiting for transfers between devices: 305 us -> 162 us
  Pallas kernels: 0 us -> 138 us
  local copies, waits for them, and re-layouts: 52.3 us -> 17.1 us
  starting transfers between devices: 28.8 us -> 0.04 us
  matrix products: 38.5 us -> 16.6 us
  blocking collectives: 90.6 us -> 78 us
    pallas_call x0 -> x1, Pallas kernels: none -> 138 us  [exchange(): pl.pallas_call(core_kernel, out_shape=(jax.ShapeDtypeStruct((80, 8, 1536)...]
    psum x1, waiting for transfers between devices: 235 us -> 162 us  [on_device(): sum_w, sum_b, sum_c = lax.psum((part_w, part_b, part_c), every)]
    all_to_all x5 -> x0, waiting for transfers between devices: 70.3 us -> none  [the longest x1 21.3 us: on_device(): lax.all_to_all(send_h.reshape(groups, -1, ffw), PLANE, 0, 0, tiled=True)]
    all_to_all x5 -> x0, starting transfers between devices: 28.7 us -> none  [the longest x1 7.5 us: on_device(): lax.all_to_all(back_rows.reshape(groups, -1, ffw), PLANE, 0, 0, tiled=True)]
    reshape x4 -> x0, local copies, waits for them, and re-layouts: 26.3 us -> none  [the longest x1 11.2 us: on_device(): weight = full.reshape(8, 2, 4, 2, 2, share, quarter).transpose(2, 4, 0, 5...]
    dot_general x3 -> x0, matrix products: 20.4 us -> none  [the longest x1 7.51 us: on_device(): lax.dot_general(got_h, weight, (((1,), (1,)), ((), ())), preferred_elemen...]
    all_to_all x1 -> x0, blocking collectives: 15.1 us -> none  [on_device(): part = lax.all_to_all(merged, PLANE, 0, 0, tiled=True)]
  transfers between devices with their start and end apart: 8 -> 1, of which waited for: 5 -> 1; matrix products, arithmetic and copies ran while one was open for 16% -> 2% of each run, Pallas kernels for 0% -> 0%
where the time goes in v2:
time: 435 us; the launch traced here: 434 us
  waiting for transfers between devices  162 us (37%)
  Pallas kernels  138 us (32%)
  blocking collectives  78 us (18%)
  local copies, waits for them, and re-layouts  17.1 us (4%)
  matrix products  16.6 us (4%)
  between operations  14.3 us (3%)
  other arithmetic  8.25 us (2%)
    psum x1, waiting for transfers between devices, on_device(): sum_w, sum_b, sum_c = lax.psum((part_w, part_b, part_c), every)  162 us
    pallas_call x1, Pallas kernels, exchange(): pl.pallas_call(core_kernel, out_shape=(jax.ShapeDtypeStruct((80, 8, 1536)...  138 us
    psum x1, blocking collectives, on_device(): sum_w, sum_b, sum_c = lax.psum((part_w, part_b, part_c), every)  78 us
  transfers between devices with their start and end apart: 1, of which 1 were waited for; matrix products, arithmetic and copies ran while one was open for 2% of the time, Pallas kernels for 0%

profile of v2, /device:TPU:1, one launch (start us, length us, event | category | flops | bytes accessed | tf_op | source)
XLA Modules:
  0.0 434.1 jit_solution(6219642187817090179)
XLA Ops:
  7.2 0.0 copy-start
  7.2 0.0 copy-start.7
  7.2 0.0 all-reduce.3.cloned.1.call-start
  7.3 0.9 fusion.21
  8.2 0.8 select_reduce_fusion.5
  9.0 0.0 copy-start.4
  9.0 0.0 copy-start.8
  9.0 1.2 constant_dynamic-slice_fusion
  10.2 0.0 copy-start.5
  10.2 0.6 gather_fusion.1
  10.8 0.6 gather_fusion.3
  11.5 0.7 gather_fusion
  12.1 0.7 gather_fusion.2
  12.8 0.1 select_reduce_fusion.2
  12.9 0.1 copy.30
  13.0 0.1 add.111
  13.1 0.3 fusion.9
  13.5 0.0 copy-done
  13.5 0.0 copy-done.4
  13.5 0.0 copy-done.8
  13.5 0.2 convolution_add_fusion
  13.8 0.1 copy.33
  13.9 0.1 div.21
  14.0 0.1 bitcast_convert_fusion
  14.1 2.2 mul.164.clone
  16.3 4.9 %mul.165 = f32[512,1536]{1,0:T(8,128)} reshape(f32[128,4,1536]{2,1,0:T(4,128)} %mul.164.clone) | data formatting | bytes 6291456 | tf_op jit(solution)/shard_map/mul | solution.py:340
  21.2 3.7 reshape.251
  24.9 0.1 convert_element_type.93
  25.0 0.1 copy.31
  25.0 0.0 copy-start.2
  25.1 4.0 fusion.1.send_h
  29.1 2.6 fusion.2.send_g
  31.7 0.9 fusion.17.wq
  32.6 137.6 %exchange.1 = (bf16[80,8,1536]{2,1,0:T(8,128)(2,1)}, bf16[80,8,1536]{2,1,0:T(8,128)(2,1)}, f32[16,3,8,384]{3,2,1,0:T(8,128)}) custom-call(bf16[16,3,8,384]{3,2,1,0:T(8,128)(2,1)} %fusion.17.wq, bf16[80,8,1536]{2,1,0:T(8,128)(2,1)} %fusion.1.send_h, bf16[80,8,1536]{2,1,0:T(8,128)(2,1)} %fusion.2.send_g), custom_call_target="tpu_custom_call" | custom-call | tf_op jit(solution)/shard_map/exchange/pallas_call | solution.py:274
  170.1 4.0 multiply_reduce_fusion
  174.2 0.1 select_reduce_fusion
  174.3 1.1 convolution_bitcast_fusion
  175.5 0.0 all-reduce.3.cloned.1.call-update
  175.5 1.3 fusion
  176.8 0.6 gather_fusion.4
  177.4 2.4 broadcast_multiply_fusion
  179.9 78.0 %all-reduce = (f32[32]{0:T(128)S(1)}, f32[32]{0:T(128)S(1)}) all-reduce(f32[32]{0:T(128)S(1)} %get-tuple-element.15, f32[32]{0:T(128)S(1)} %get-tuple-element.22), channel_id=1, replica_groups=mesh['x'=4,'yl'=2,'z'=8,'yh'=2,'c'=2] {'x','yl','z','yh','c'}, use_global_device_ids=true, to_apply=%region_13.14 | all-reduce | flops 64 | bytes 512 | tf_op jit(solution)/shard_map/psum | solution.py:393
  257.9 0.5 broadcast_multiply_fusion.3
  258.4 3.0 convolution_convert_fusion.3
  261.4 1.3 reshape.256
  262.7 0.5 broadcast_multiply_fusion.4
  263.2 162.3 %all-reduce.3.cloned.1.call-done = f32[2880,32]{0,1:T(8,128)} async-done(((f32[2880,32]{0,1:T(8,128)}), f32[2880,32]{0,1:T(8,128)}) %all-reduce.3.cloned.1.call-update) | async-done | bytes 368656 | tf_op jit(solution)/shard_map/psum | solution.py:393
  425.5 1.8 broadcast_multiply_fusion.1
  (26 shorter events, 0.2 us)
Async XLA Ops:
  7.2 6.3 %copy-start = (bf16[1,128,2880]{1,2,0:T(8,128)(2,1)S(1)}, bf16[1,128,2880]{1,2,0:T(8,128)(2,1)}, u32[]{:S(2)}) copy-start(bf16[1,128,2880]{1,2,0:T(8,128)(2,1)} %param.9) | copy-start | bytes 2211844
  7.2 5.6 %copy-start.7 = (s32[32]{0:T(128)S(1)}, s32[32]{0:T(128)}, u32[]{:S(2)}) copy-start(s32[32]{0:T(128)} %param.14) | copy-start | bytes 388
  7.2 4.3 copy-start.1
  7.2 5.6 %copy-start.6 = (s32[1,128,4]{1,2,0:T(4,128)S(1)}, s32[1,128,4]{1,2,0:T(4,128)}, u32[]{:S(2)}) copy-start(s32[1,128,4]{1,2,0:T(4,128)} %param.13) | copy-start | bytes 6148
  7.2 418.3 %all-reduce.3.cloned.1.call-start = ((), (), s32[]{:S(2)}) async-start(), calls=%async_computation | async-start | bytes 753664 | tf_op jit(solution)/shard_map/psum | solution.py:393
  9.0 4.5 %copy-start.4 = (bf16[2880,32]{0,1:T(8,128)(2,1)S(1)}, bf16[2880,32]{0,1:T(8,128)(2,1)}, u32[]{:S(2)}) copy-start(bf16[2880,32]{0,1:T(8,128)(2,1)} %param.10) | copy-start | bytes 552964
  9.0 4.5 %copy-start.8 = (f32[32]{0:T(128)S(1)}, f32[32]{0:T(128)}, u32[]{:S(2)}) copy-start(f32[32]{0:T(128)} %param.11) | copy-start | bytes 388
  10.2 3.8 copy-start.5
  25.0 4.0 copy-start.2
  174.2 2.6 copy-start.3
Sparse Core Ops, SparseCore 0:
  175.6 249.8 all-reduce.2

commit v3 on v2

--- a/solution.py
+++ b/solution.py
@@ -300,6 +300,91 @@
         ),
         name="exchange",
     )(wq, send_h, send_g)
+
+
+def reduce_kernel(table, total, first, mine, second, done, p_s, p_r, q_s, q_r, t_s, t_r):
+    x, yl, z = lax.axis_index("x"), lax.axis_index("yl"), lax.axis_index("z")
+    yh, c = lax.axis_index("yh"), lax.axis_index("c")
+    y = yh * 2 + yl
+    me = x * 4 + y
+    zc = z * 2 + c
+
+    def line(k):
+        oz = lax.rem(z + k // 2, 8)
+        oc = lax.rem(c + lax.rem(k, 2), 2)
+        return {"z": oz, "c": oc}
+
+    def spot(px, py):
+        return (
+            pl.ds(pl.multiple_of(8 * px, 8), 8),
+            pl.ds(pl.multiple_of(768 * py, 768), 768),
+        )
+
+    def each(do):
+        def step(k, carry):
+            do(k)
+            return carry
+
+        lax.fori_loop(1, 16, step, 0)
+
+    barrier = pltpu.get_barrier_semaphore()
+
+    def greet(k):
+        px, py = offset(k, x, y)
+        pl.semaphore_signal(barrier, inc=1, device_id=plane_id(px, py), device_id_type=MESH)
+        pl.semaphore_signal(barrier, inc=1, device_id=line(k), device_id_type=MESH)
+
+    each(greet)
+    pl.semaphore_wait(barrier, 30)
+
+    def p_copy(k):
+        px, py = offset(k, x, y)
+        return remote(
+            table.at[spot(px, py)], first.at[me], p_s.at[k], p_r.at[k], plane_id(px, py)
+        )
+
+    def q_copy(k):
+        return remote(mine, second.at[zc], q_s.at[k], q_r.at[k], line(k))
+
+    def t_copy(k):
+        px, py = offset(k, x, y)
+        return remote(
+            done, total.at[spot(x, y)], t_s.at[k], t_r.at[k], plane_id(px, py)
+        )
+
+    each(lambda k: p_copy(k).start())
+    first[me] = table[spot(x, y)]
+    each(lambda k: p_copy(k).wait_recv())
+    mine[...] = jnp.sum(first[...], axis=0)
+    each(lambda k: q_copy(k).start())
+    second[zc] = mine[...]
+    each(lambda k: q_copy(k).wait_recv())
+    done[...] = jnp.sum(second[...], axis=0)
+    each(lambda k: t_copy(k).start())
+    total[spot(x, y)] = done[...]
+    each(lambda k: p_copy(k).wait_send())
+    each(lambda k: q_copy(k).wait_send())
+    each(lambda k: t_copy(k).wait())
+
+
+def reduce_all(table):
+    vmem = pl.BlockSpec(memory_space=pltpu.VMEM)
+    dma = pltpu.SemaphoreType.DMA((16,))
+    return pl.pallas_call(
+        reduce_kernel,
+        out_shape=jax.ShapeDtypeStruct((32, 3072), F32),
+        in_specs=[vmem],
+        out_specs=vmem,
+        scratch_shapes=[
+            pltpu.VMEM((16, 8, 768), F32),
+            pltpu.VMEM((8, 768), F32),
+            pltpu.VMEM((16, 8, 768), F32),
+            pltpu.VMEM((8, 768), F32),
+            dma, dma, dma, dma, dma, dma,
+        ],
+        compiler_params=pltpu.CompilerParams(collective_id=1, has_side_effects=True),
+        name="reduce_all",
+    )(table)
 
 
 def on_device(
@@ -382,22 +467,30 @@
         logit_half, router_w, (((1,), (1,)), ((), ())), preferred_element_type=jnp.float32
     ).astype(jnp.bfloat16)
     part_w = lax.dot_general(
-        x, logit_half, (((0,), (0,)), ((), ())), preferred_element_type=jnp.float32
+        logit_half, x, (((0,), (0,)), ((), ())), preferred_element_type=jnp.float32
     )
     part_b = jnp.sum(logit_grad, axis=0)
     source_grad = merged_grad[merge_map]
     mine_out = lax.dynamic_slice_in_dim(source_w, (yh * 2 + c) * quarter, quarter, 2)
     part_c = jnp.sum(source_grad * mine_out.astype(jnp.float32), axis=(1, 2))
     source_w_grad = source_grad * (merge_coef * grad_scale)[:, None, None]
-    every = ("x", "yl", "z", "yh", "c")
-    sum_w, sum_b, sum_c = lax.psum((part_w, part_b, part_c), every)
+    table = jnp.concatenate(
+        [
+            part_w,
+            part_b[:, None],
+            part_c[:, None],
+            jnp.zeros((experts, 3072 - feat - 2), jnp.float32),
+        ],
+        axis=1,
+    )
+    total = reduce_all(table) * grad_scale
     return (
         mixed.reshape(1, tok, dw),
         hidden_grad,
         token_grad.reshape(1, tok, feat),
-        sum_w * grad_scale,
-        sum_b * grad_scale,
-        sum_c * grad_scale,
+        total[:, :feat].T,
+        total[:, feat],
+        total[:, feat + 1],
         source_w_grad,
     )
 

time: 435 us -> 218 us (0.50)
  waiting for transfers between devices: 162 us -> 0 us
  blocking collectives: 78 us -> 0 us
  Pallas kernels: 138 us -> 172 us
  between operations: 14.3 us -> 0.89 us
    psum x1 -> x0, waiting for transfers between devices: 162 us -> none  [on_device(): sum_w, sum_b, sum_c = lax.psum((part_w, part_b, part_c), every)]
    psum x1 -> x0, blocking collectives: 78 us -> none  [on_device(): sum_w, sum_b, sum_c = lax.psum((part_w, part_b, part_c), every)]
    pallas_call x0 -> x1, Pallas kernels: none -> 34.3 us  [reduce_all(): pl.pallas_call(reduce_kernel, out_shape=jax.ShapeDtypeStruct((32, 3072),...]
  transfers between devices with their start and end apart: 1 -> 0, of which waited for: 1 -> 0; matrix products, arithmetic and copies ran while one was open for 2% -> 0% of each run, Pallas kernels for 0% -> 0%
where the time goes in v3:
time: 218 us; the launch traced here: 217 us
  Pallas kernels  172 us (79%)
  local copies, waits for them, and re-layouts  20 us (9%)
  matrix products  17.5 us (8%)
  other arithmetic  6.51 us (3%)
    pallas_call x1, Pallas kernels, exchange(): pl.pallas_call(core_kernel, out_shape=(jax.ShapeDtypeStruct((80, 8, 1536)...  138 us
    pallas_call x1, Pallas kernels, reduce_all(): pl.pallas_call(reduce_kernel, out_shape=jax.ShapeDtypeStruct((32, 3072),...  34.3 us
    mul x2, local copies, waits for them, and re-layouts, on_device(): gate[:, :, None] * og[:, None, :]  7.07 us
    dot_general x1, matrix products, on_device(): jnp.dot(select, slot_grad, preferred_element_type=jnp.float32)  4.43 us

profile of v3, /device:TPU:1, one launch (start us, length us, event | category | flops | bytes accessed | tf_op | source)
XLA Modules:
  0.0 217.1 jit_solution(15953065874155091345)
XLA Ops:
  0.6 0.0 copy-start
  0.6 0.0 copy-start.1
  0.7 0.0 copy-start.5
  0.7 0.0 copy-start.6
  0.7 1.2 constant_dynamic-slice_fusion
  1.9 0.0 copy-start.3
  1.9 0.0 copy-start.7
  1.9 0.9 fusion.22
  2.8 0.8 select_reduce_fusion.5
  3.6 0.6 gather_fusion.1
  4.3 0.6 gather_fusion.3
  4.9 0.0 copy-done.1
  4.9 0.0 copy-start.4
  4.9 0.7 gather_fusion
  5.6 0.7 gather_fusion.2
  6.2 0.9 fusion.18.wq
  7.1 0.1 select_reduce_fusion.2
  7.2 0.1 copy.36
  7.4 0.1 add.105
  7.5 0.3 fusion.9
  7.8 0.2 convolution_add_fusion
  8.1 0.1 copy.39
  8.2 0.1 div.21
  8.3 0.1 bitcast_convert_fusion
  8.4 2.2 %mul.161.clone = f32[128,4,1536]{2,1,0:T(4,128)} broadcast(f32[128,1536]{1,0:T(8,128)S(1)} %bitcast_convert_fusion), dimensions={0,2} | broadcast | bytes 3932160 | tf_op jit(solution)/shard_map/mul | solution.py:425
  10.6 4.9 %mul.162 = f32[512,1536]{1,0:T(8,128)} reshape(f32[128,4,1536]{2,1,0:T(4,128)} %mul.161.clone) | data formatting | bytes 6291456 | tf_op jit(solution)/shard_map/mul | solution.py:425
  15.5 4.4 %fusion.2.send_g = bf16[80,8,1536]{2,1,0:T(8,128)(2,1)} fusion(f32[512,1536]{1,0:T(8,128)} %mul.162, f32[512]{0:T(512)S(1)} %div.21, s32[512]{0:T(512)S(1)} %add_select_fusion), kind=kOutput, calls=%fused_computation.14 | convolution fusion | flops 1009516544 | bytes 5115904 | tf_op jit(solution)/shard_map/dot_general | solution.py:427
  19.9 3.7 %reshape.251 = bf16[512,1536]{1,0:T(8,128)(2,1)} reshape(bf16[1,128,4,1536]{3,2,1,0:T(4,128)(2,1)} %param.12) | data formatting | bytes 3145728 | tf_op jit(solution)/shard_map/reshape | solution.py:406
  23.6 3.9 %fusion.1.send_h = bf16[80,8,1536]{2,1,0:T(8,128)(2,1)} fusion(bf16[512,1536]{1,0:T(8,128)(2,1)} %reshape.251, s32[512]{0:T(512)S(1)} %add_select_fusion), kind=kOutput, calls=%fused_computation.13 | convolution fusion | flops 1007943680 | bytes 3540992 | tf_op jit(solution)/shard_map/dot_general | solution.py:426
  27.5 137.8 %exchange.1 = (bf16[80,8,1536]{2,1,0:T(8,128)(2,1)}, bf16[80,8,1536]{2,1,0:T(8,128)(2,1)}, f32[16,3,8,384]{3,2,1,0:T(8,128)}) custom-call(bf16[16,3,8,384]{3,2,1,0:T(8,128)(2,1)} %fusion.18.wq, bf16[80,8,1536]{2,1,0:T(8,128)(2,1)} %fusion.1.send_h, bf16[80,8,1536]{2,1,0:T(8,128)(2,1)} %fusion.2.send_g), custom_call_target="tpu_custom_call" | custom-call | tf_op jit(solution)/shard_map/exchange/pallas_call | solution.py:274
  165.3 0.1 convert_element_type.93
  165.4 0.1 copy.37
  165.5 4.1 %multiply_reduce_fusion = (f32[128,4]{0,1:T(4,128)S(1)}, bf16[128,1536]{1,0:T(8,128)(2,1)}) fusion(f32[128,1536]{1,0:T(8,128)S(1)} %bitcast_convert_fusion, f32[128,4]{0,1:T(4,128)S(1)} %exponential_divide_fusion, bf16[80,8,1536]{2,1,0:T(8,128)(2,1)} %get-tuple-element.10, s32[128,4]{0,1:T(4,128)S(1)} %add_select_fusion.1), kind=kOutput, calls=%fused_computation.9 | convolution fusion | flops 1009909248 | bytes 3151872 | tf_op jit(solution)/shard_map/dot_general | solution.py:454
  169.6 0.1 select_reduce_fusion
  169.7 0.4 fusion.10
  170.1 0.1 copy.41
  170.2 0.4 copy-done.2
  170.6 0.6 gather_fusion.4
  171.3 2.4 %broadcast_multiply_fusion = (f32[32,24,384]{2,1,0:T(8,128)}, f32[32]{0:T(128)S(1)}) fusion(f32[32,24,384]{2,1,0:T(8,128)S(1)} %gather_fusion.4, f32[32]{0:T(128)S(1)} %broadcast_multiply_fusion.2, bf16[32,24,1536]{2,1,0:T(8,128)(2,1)} %param.16, s32[]{:T(128)S(6)} %select_n.78), kind=kLoop, calls=%fused_computation.39 | loop fusion | flops 1179616 | bytes 2949380 | tf_op jit(solution)/shard_map/mul | solution.py:476
  173.7 0.1 copy.42
  173.8 0.8 concatenate.3.table
  174.6 34.3 %reduce_all.1 = f32[32,3072]{1,0:T(8,128)} custom-call(f32[32,3072]{1,0:T(8,128)} %concatenate.3.table), custom_call_target="tpu_custom_call" | custom-call | tf_op jit(solution)/shard_map/reduce_all/pallas_call | solution.py:373
  209.0 1.0 broadcast_multiply_fusion.1
  210.0 0.8 slice_bitcast_fusion
  210.8 0.7 slice_reduce_fusion
  211.5 1.3 fusion
  212.8 3.0 %convolution_convert_fusion.3 = bf16[512,1536]{1,0:T(8,128)(2,1)S(1)} fusion(bf16[80,8,1536]{2,1,0:T(8,128)(2,1)} %get-tuple-element.11, s32[512]{0:T(512)S(1)} %add_select_fusion), kind=kOutput, calls=%fused_computation.12 | convolution fusion | flops 1007747072 | bytes 3540992 | tf_op jit(solution)/shard_map/dot_general | solution.py:457
  215.8 1.3 reshape.256
  (25 shorter events, 0.2 us)
Async XLA Ops:
  0.6 7.1 %copy-start = (bf16[1,128,2880]{1,2,0:T(8,128)(2,1)S(1)}, bf16[1,128,2880]{1,2,0:T(8,128)(2,1)}, u32[]{:S(2)}) copy-start(bf16[1,128,2880]{1,2,0:T(8,128)(2,1)} %param.9) | copy-start | bytes 2211844
  0.6 4.2 %copy-start.1 = (f32[32]{0:T(128)S(1)}, f32[32]{0:T(128)}, u32[]{:S(2)}) copy-start(f32[32]{0:T(128)} %param.15) | copy-start | bytes 388
  0.7 6.5 %copy-start.5 = (s32[1,128,4]{1,2,0:T(4,128)S(1)}, s32[1,128,4]{1,2,0:T(4,128)}, u32[]{:S(2)}) copy-start(s32[1,128,4]{1,2,0:T(4,128)} %param.13) | copy-start | bytes 6148
  0.7 6.5 %copy-start.6 = (s32[32]{0:T(128)S(1)}, s32[32]{0:T(128)}, u32[]{:S(2)}) copy-start(s32[32]{0:T(128)} %param.14) | copy-start | bytes 388
  1.9 5.9 %copy-start.3 = (bf16[2880,32]{0,1:T(8,128)(2,1)S(1)}, bf16[2880,32]{0,1:T(8,128)(2,1)}, u32[]{:S(2)}) copy-start(bf16[2880,32]{0,1:T(8,128)(2,1)} %param.10) | copy-start | bytes 552964
  1.9 5.9 %copy-start.7 = (f32[32]{0:T(128)S(1)}, f32[32]{0:T(128)}, u32[]{:S(2)}) copy-start(f32[32]{0:T(128)} %param.11) | copy-start | bytes 388
  4.9 3.5 %copy-start.4 = (bf16[1,128,1536]{2,1,0:T(8,128)(2,1)S(1)}, bf16[1,128,1536]{2,1,0:T(8,128)(2,1)}, u32[]{:S(2)}) copy-start(bf16[1,128,1536]{2,1,0:T(8,128)(2,1)} %param.17) | copy-start | bytes 1179652
  169.6 1.1 copy-start.2

commit v4 on v2

v4 whole, which is shorter than its diff:
```python
import math

import jax
import jax.numpy as jnp
from jax import lax
from jax.experimental import pallas as pl
from jax.experimental.pallas import tpu as pltpu
from jax.sharding import PartitionSpec as P

MESH = pl.DeviceIdType.MESH
BF = jnp.bfloat16
F32 = jnp.float32
CAP = 10
TOP = 4
ROWS = 640
SLOTS = 512
TOK = 128
WIDE = 1536
EXPERTS = 32
FEAT = 2880


def offset(k, x, y):
    px = lax.rem(x + k // 4, 4)
    py = lax.rem(y + lax.rem(k, 4), 4)
    return px, py


def plane_id(px, py):
    return {"x": px, "yl": lax.rem(py, 2), "yh": py // 2}


def remote(src, dst, send, recv, where):
    return pltpu.make_async_remote_copy(
        src_ref=src, dst_ref=dst, send_sem=send, recv_sem=recv, device_id=where,
        device_id_type=MESH,
    )


def spot(px, py):
    return (
        pl.ds(pl.multiple_of(8 * px, 8), 8),
        pl.ds(pl.multiple_of(768 * py, 768), 768),
    )


def each(do):
    def step(k, carry):
        do(k)
        return carry

    lax.fori_loop(1, 16, step, 0)


def iota(shape, dim):
    return lax.broadcasted_iota(jnp.int32, shape, dim)


def group_sum(v, lane):
    n = v.shape[1]
    v = v + jnp.where(lane % 2 == 0, pltpu.roll(v, n - 1, 1), pltpu.roll(v, 1, 1))
    return v + jnp.where(lane % 4 < 2, pltpu.roll(v, n - 2, 1), pltpu.roll(v, 2, 1))


def exact(a, b, dims):
    return lax.dot_general(
        a, b, (dims, ((), ())), precision=lax.Precision.HIGHEST, preferred_element_type=F32
    )


def kernel(
    grad_scale,
    tokens, router_t, bias, hid, idx, map_row, og, map_s, coef_s, source,
    mixed, hidden_grad, token_grad, total, small, expert_grad,
    src_a, src_b, wq, sel, og_rows, gate_s, pick_s, send_h, send_g,
    weight, recv_h, recv_g, mat_h, mat_g, mat_w, home_out, home_back,
    part, sib, ring_send, ring_recv, last, got,
    table, first, mine, second, done, row_a, row_b, row_c, row_d,
    l_sem,
    a_s, a_r, h_s, h_r, g_s, g_r, zp_s, zp_r, zm_s, zm_r, w_s, w_r,
    o_s, o_r, b_s, b_r, e_s, e_r, rp_s, rp_r, rm_s, rm_r, l_s, l_r,
    p_s, p_r, q_s, q_r, t_s, t_r, u_s, u_r, v_s, v_r,
):
    x, yl, z = lax.axis_index("x"), lax.axis_index("yl"), lax.axis_index("z")
    yh, c = lax.axis_index("yh"), lax.axis_index("c")
    y = yh * 2 + yl
    me = x * 4 + y
    xy = x * 2 + yl
    zc = z * 2 + c
    up, down = lax.rem(z + 1, 8), lax.rem(z + 7, 8)
    sibling = {"c": 1 - c}

    def line(k):
        return {"z": lax.rem(z + k // 2, 8), "c": lax.rem(c + lax.rem(k, 2), 2)}

    quarter = pl.ds(pl.multiple_of((c * 2 + yh) * 384, 384), 384)
    owned = pl.ds(pl.multiple_of((yh * 2 + c) * 384, 384), 384)
    half = pl.ds(pl.multiple_of(c * 768, 768), 768)
    load_a = pltpu.make_async_copy(source.at[:, :, :, quarter], src_a, l_sem.at[0])
    load_b = pltpu.make_async_copy(source.at[:, :, :, owned], src_b, l_sem.at[1])
    load_a.start()

    barrier = pltpu.get_barrier_semaphore()

    def greet(k):
        px, py = offset(k, x, y)
        pl.semaphore_signal(barrier, inc=1, device_id=plane_id(px, py), device_id_type=MESH)
        pl.semaphore_signal(barrier, inc=1, device_id=line(k), device_id_type=MESH)

    each(greet)

    lane = iota((1, SLOTS), 1)
    token_of = (iota((SLOTS, TOK), 0) // TOP == iota((SLOTS, TOK), 1)).astype(F32)
    ids = lax.dot_general(
        idx[...].astype(F32).astype(BF), token_of.astype(BF), (((1,), (1,)), ((), ())),
        preferred_element_type=F32,
    )
    idx_row = jnp.sum(
        jnp.where(iota((TOP, SLOTS), 0) == lane % TOP, ids, 0.0), axis=0, keepdims=True
    ).astype(jnp.int32)
    pick = iota((EXPERTS, SLOTS), 0) == idx_row
    square = iota((EXPERTS, EXPERTS), 0) == iota((EXPERTS, EXPERTS), 1)
    map_col = jnp.sum(
        jnp.where(square, map_row[...].astype(F32), 0.0), axis=1, keepdims=True
    )
    merged_row = jnp.sum(
        jnp.where(pick, map_col, 0.0), axis=0, keepdims=True
    ).astype(jnp.int32)
    lane_row = merged_row * 4 + (lane // TOP) % 4
    spread = iota((64, SLOTS), 0) == lane_row
    earlier = (iota((SLOTS, SLOTS), 0) < iota((SLOTS, SLOTS), 1)).astype(F32).astype(BF)
    before = jnp.dot(spread.astype(F32).astype(BF), earlier, preferred_element_type=F32)
    rank = jnp.sum(jnp.where(spread, before, 0.0), axis=0, keepdims=True).astype(jnp.int32)
    index_row = jnp.where(rank < CAP, lane_row * CAP + rank, ROWS)
    sel[...] = (iota((ROWS, SLOTS), 0) == index_row).astype(F32).astype(BF)
    pick_s[...] = pick.astype(F32)

    def pack_h(j, carry):
        span = pl.ds(pl.multiple_of(j * 256, 256), 256)
        tile = jnp.dot(sel[...], hid[:, span], preferred_element_type=F32)
        send_h[:, :, span] = tile.reshape(80, 8, 256).astype(BF)
        return carry

    lax.fori_loop(0, 6, pack_h, 0)

    load_a.wait()
    load_b.start()

    def merge(g, carry):
        one, two = jnp.int32(0), jnp.int32(0)
        for e in range(EXPERTS):
            two = jnp.where(map_s[e] == g, e, two)
        for e in reversed(range(EXPERTS)):
            one = jnp.where(map_s[e] == g, e, one)
        wq[g] = (
            coef_s[one] * src_a[one].astype(F32) + coef_s[two] * src_a[two].astype(F32)
        ).astype(BF)
        return carry

    lax.fori_loop(0, 16, merge, 0)
    pl.semaphore_wait(barrier, 30)

    def plane_copy(k, src, dst, send, recv):
        px, py = offset(k, x, y)
        return remote(
            src.at[pl.ds(5 * (px * 4 + py), 5)], dst.at[pl.ds(5 * me, 5)],
            send.at[k], recv.at[k], plane_id(px, py),
        )

    def a_copy(k):
        px, py = offset(k, x, y)
        return remote(
            wq.at[px * 4 + py], weight.at[xy, z, :, :, quarter], a_s.at[k], a_r.at[k],
            plane_id(px, py),
        )

    def h_copy(k):
        return plane_copy(k, send_h, recv_h, h_s, h_r)

    def g_copy(k):
        return plane_copy(k, send_g, recv_g, g_s, g_r)

    def o_copy(k):
        return plane_copy(k, send_h, home_out, o_s, o_r)

    def b_copy(k, n):
        px, py = offset(k, x, y)
        cols = pl.ds(n * 768, 768)
        return remote(
            send_g.at[pl.ds(5 * (px * 4 + py), 5), :, cols],
            home_back.at[pl.ds(5 * me, 5), :, cols],
            b_s.at[n, k], b_r.at[n, k], plane_id(px, py),
        )

    def l_copy(k):
        px, py = offset(k, x, y)
        return remote(
            last.at[py // 2, px * 2 + lax.rem(py, 2)], got.at[me],
            l_s.at[k], l_r.at[k], plane_id(px, py),
        )

    each(lambda k: a_copy(k).start())
    each(lambda k: h_copy(k).start())
    own = pl.ds(5 * me, 5)
    weight[xy, z, :, :, quarter] = wq[me]
    recv_h[own] = send_h[own]

    logits = jnp.dot(
        router_t[...], tokens[...], preferred_element_type=F32
    ) + jnp.sum(jnp.where(square, bias[...], 0.0), axis=1, keepdims=True)
    wide = exact(logits, token_of, ((1,), (1,)))
    chosen = jnp.sum(jnp.where(pick, wide, 0.0), axis=0, keepdims=True)
    raised = jnp.exp(chosen)
    gate = raised / group_sum(raised, lane)
    gate_s[...] = gate
    gate_col = jnp.sum(jnp.where(sel[...] > 0, gate, 0.0), axis=1, keepdims=True)
    row_token = jnp.dot(sel[...], token_of.astype(BF), preferred_element_type=F32).astype(BF)
    for j in range(6):
        span = pl.ds(j * 256, 256)
        tile = jnp.dot(row_token, og[:, span], preferred_element_type=F32)
        og_rows[:, span] = tile.astype(BF)
        send_g[:, :, span] = (tile * gate_col).reshape(80, 8, 256).astype(BF)
    each(lambda k: g_copy(k).start())
    recv_g[own] = send_g[own]

    each(lambda k: a_copy(k).wait_recv())

    def block(b):
        return weight.at[:, b, :, :, half]

    def w_copy(i):
        b = lax.rem(z + 8 - i, 8) if i <= 4 else lax.rem(z + i - 4, 8)
        return remote(block(b), block(b), w_s.at[i], w_r.at[i], sibling)

    def zp_copy(s):
        b = lax.rem(z + 8 - s, 8)
        return remote(block(b), block(b), zp_s.at[s], zp_r.at[s], {"z": up})

    def zm_copy(s):
        b = lax.rem(z + s, 8)
        return remote(block(b), block(b), zm_s.at[s], zm_r.at[s], {"z": down})

    zp_copy(0).start()
    zm_copy(0).start()
    w_copy(0).start()
    for s in range(4):
        zp_copy(s).wait_recv()
        if s < 3:
            zp_copy(s + 1).start()
        w_copy(s + 1).start()
        if s < 3:
            zm_copy(s).wait_recv()
            if s < 2:
                zm_copy(s + 1).start()
            w_copy(s + 5).start()

    def reshape_rows(src, dst):
        def step(i, carry):
            dst[pl.ds(pl.multiple_of(i * 80, 80), 80), :] = (
                src[pl.ds(i * 10, 10)].astype(F32).reshape(80, WIDE).astype(BF)
            )
            return carry

        lax.fori_loop(0, 8, step, 0)

    each(lambda k: h_copy(k).wait_recv())
    reshape_rows(recv_h, mat_h)
    for i in range(8):
        w_copy(i).wait_recv()

    def shape_w(i, carry):
        mat_w[pl.ds(pl.multiple_of(i * 192, 192), 192), :] = (
            weight[i].astype(F32).reshape(192, WIDE).astype(BF)
        )
        return carry

    lax.fori_loop(0, 8, shape_w, 0)
    each(lambda k: h_copy(k).wait_send())

    def forward(j, carry):
        span = pl.ds(pl.multiple_of(j * 256, 256), 256)
        tile = lax.dot_general(
            mat_h[...], mat_w[span, :], (((1,), (1,)), ((), ())), preferred_element_type=F32
        )
        send_h[:, :, span] = tile.reshape(80, 8, 256).astype(BF)
        return carry

    lax.fori_loop(0, 6, forward, 0)
    each(lambda k: o_copy(k).start())
    home_out[own] = send_h[own]
    each(lambda k: g_copy(k).wait_recv())
    reshape_rows(recv_g, mat_g)

    def outer(i, carry):
        cols = pl.ds(pl.multiple_of(i * 384, 384), 384)
        tile = lax.dot_general(
            mat_g[:, cols], mat_h[...], (((0,), (0,)), ((), ())), preferred_element_type=F32
        )
        part[pl.ds(i * 2, 2)] = tile.reshape(2, 8, 3, 8, WIDE).astype(BF)
        return carry

    lax.fori_loop(0, 4, outer, 0)

    def e_copy(h):
        there = pl.ds(pl.multiple_of(h * 768 + (1 - c) * 384, 384), 384)
        return remote(
            part.at[:, :, :, :, there], sib.at[h], e_s.at[h], e_r.at[h], sibling
        )

    for h in range(2):
        e_copy(h).start()
    each(lambda k: g_copy(k).wait_send())

    def backward(j, carry):
        span = pl.ds(pl.multiple_of(j * 256, 256), 256)
        tile = jnp.dot(mat_g[...], mat_w[:, span], preferred_element_type=F32)
        send_g[:, :, span] = tile.reshape(80, 8, 256).astype(BF)
        return carry

    def local(h, b):
        here = pl.ds(pl.multiple_of(h * 768 + c * 384, 384), 384)
        return part[:, b, :, :, here].astype(F32) + sib[h, :, b].astype(F32)

    def ring(h, s):
        if h == 0:
            return remote(
                ring_send.at[0, s], ring_recv.at[0, s], rp_s.at[s], rp_r.at[s], {"z": up}
            )
        return remote(
            ring_send.at[1, s], ring_recv.at[1, s], rm_s.at[s], rm_r.at[s], {"z": down}
        )

    def ring_step(s):
        for h in range(2):
            b = lax.rem(z + 15 - s, 8) if h == 0 else lax.rem(z + 1 + s, 8)
            value = local(h, b)
            if s > 0:
                ring(h, s - 1).wait_recv()
                value = value + ring_recv[h, s - 1].astype(F32)
            ring_send[h, s] = value.astype(BF)
            ring(h, s).start()

    lax.fori_loop(0, 3, backward, 0)
    each(lambda k: b_copy(k, 0).start())
    for h in range(2):
        e_copy(h).wait_recv()
    ring_step(0)
    lax.fori_loop(3, 6, backward, 0)
    each(lambda k: b_copy(k, 1).start())
    home_back[own] = send_g[own]
    for s in range(1, 7):
        ring_step(s)
    load_b.wait()
    for h in range(2):
        value = local(h, z)
        ring(h, 6).wait_recv()
        last[h] = (value + ring_recv[h, 6].astype(F32)).astype(BF)
    each(lambda k: l_copy(k).start())
    got[me] = last[yh, xy]

    each(lambda k: o_copy(k).wait_recv())

    def score_rows(i, carry):
        rows = pl.ds(pl.multiple_of(i * 80, 80), 80)
        value = home_out[pl.ds(i * 10, 10)].astype(F32).reshape(80, WIDE)
        mat_h[rows, :] = value.astype(BF)
        score = jnp.sum(value * og_rows[rows, :].astype(F32), axis=1, keepdims=True)
        return carry + jnp.sum(
            jnp.where(sel[rows, :] > 0, score, 0.0), axis=0, keepdims=True
        )

    score_row = lax.fori_loop(0, 8, score_rows, jnp.zeros((1, SLOTS), F32))
    gate = gate_s[...]
    chosen_grad = gate * (score_row - group_sum(gate * score_row, lane))
    slot_table = jnp.where(pick_s[...] > 0, chosen_grad, 0.0)
    logit_grad = exact(slot_table, token_of, ((1,), (0,)))
    logit_half = logit_grad.astype(BF)
    bias_col = jnp.sum(logit_grad, axis=1, keepdims=True)
    table[:, pl.ds(2816, 256)] = jnp.zeros((EXPERTS, 256), F32)
    table[:, pl.ds(0, FEAT)] = lax.dot_general(
        logit_half, tokens[...], (((1,), (1,)), ((), ())), preferred_element_type=F32
    )

    def p_copy(k):
        px, py = offset(k, x, y)
        return remote(
            table.at[spot(px, py)], first.at[me], p_s.at[k], p_r.at[k], plane_id(px, py)
        )

    def q_copy(k):
        return remote(mine, second.at[zc], q_s.at[k], q_r.at[k], line(k))

    def t_copy(k):
        px, py = offset(k, x, y)
        return remote(
            done, total.at[spot(x, y)], t_s.at[k], t_r.at[k], plane_id(px, py)
        )

    each(lambda k: p_copy(k).start())
    first[me] = table[spot(x, y)]
    each(lambda k: l_copy(k).wait_recv())

    def coefficient(e, carry):
        grad = got[map_s[e]].astype(F32)
        prod = jnp.sum(jnp.sum(grad * src_b[e].astype(F32), axis=0), axis=0, keepdims=True)
        dot = jnp.sum(prod, axis=1, keepdims=True)
        return carry + jnp.where(iota((1, 128), 1) == e, dot, 0.0)

    coef_row = lax.fori_loop(0, EXPERTS, coefficient, jnp.zeros((1, 128), F32))
    bias_row = jnp.sum(
        jnp.where(iota((EXPERTS, 128), 1) - 32 == iota((EXPERTS, 128), 0), bias_col, 0.0),
        axis=0, keepdims=True,
    )
    row_a[...] = jnp.broadcast_to(coef_row + bias_row, (8, 128))

    def u_copy(k):
        px, py = offset(k, x, y)
        return remote(row_a, row_b.at[me], u_s.at[k], u_r.at[k], plane_id(px, py))

    def v_copy(k):
        return remote(row_c, row_d.at[zc], v_s.at[k], v_r.at[k], line(k))

    each(lambda k: u_copy(k).start())
    row_b[me] = row_a[...]

    each(lambda k: p_copy(k).wait_recv())
    mine[...] = jnp.sum(first[...], axis=0)
    each(lambda k: q_copy(k).start())
    second[zc] = mine[...]

    def expert(e, carry):
        expert_grad[e] = got[map_s[e]].astype(F32) * (coef_s[e] * grad_scale)
        return carry

    lax.fori_loop(0, EXPERTS, expert, 0)
    each(lambda k: u_copy(k).wait_recv())
    row_c[...] = jnp.sum(row_b[...], axis=0)
    each(lambda k: v_copy(k).start())
    row_d[zc] = row_c[...]
    token_grad[...] = lax.dot_general(
        router_t[...], logit_half, (((0,), (0,)), ((), ())), preferred_element_type=F32
    ).astype(BF)
    each(lambda k: q_copy(k).wait_recv())
    done[...] = jnp.sum(second[...], axis=0) * grad_scale
    each(lambda k: t_copy(k).start())
    total[spot(x, y)] = done[...]
    slot_token = iota((TOK, SLOTS), 1) // TOP == iota((TOK, SLOTS), 0)
    spread_gate = jnp.where(slot_token, gate, 0.0)
    high = spread_gate.astype(BF)
    low = (spread_gate - high.astype(F32)).astype(BF)

    def over_rows(v):
        return lax.dot_general(
            v, sel[...], (((1,), (1,)), ((), ())), preferred_element_type=F32
        ).astype(BF)

    mixed[...] = (
        jnp.dot(over_rows(high), mat_h[...], preferred_element_type=F32)
        + jnp.dot(over_rows(low), mat_h[...], preferred_element_type=F32)
    ).astype(BF)
    for n in range(2):
        each(lambda k: b_copy(k, n).wait_recv())
    reshape_rows(home_back, mat_g)
    for j in range(6):
        span = pl.ds(j * 256, 256)
        hidden_grad[:, span] = lax.dot_general(
            sel[...], mat_g[:, span], (((0,), (0,)), ((), ())), preferred_element_type=F32
        ).astype(BF)
    each(lambda k: v_copy(k).wait_recv())
    small[...] = jnp.sum(row_d[...], axis=0) * grad_scale
    each(lambda k: t_copy(k).wait_recv())

    each(lambda k: a_copy(k).wait_send())
    for s in range(4):
        zp_copy(s).wait_send()
    for s in range(3):
        zm_copy(s).wait_send()
    for i in range(8):
        w_copy(i).wait_send()
    for h in range(2):
        e_copy(h).wait_send()
        for s in range(7):
            ring(h, s).wait_send()
    each(lambda k: o_copy(k).wait_send())
    for n in range(2):
        each(lambda k: b_copy(k, n).wait_send())
    each(lambda k: l_copy(k).wait_send())
    each(lambda k: p_copy(k).wait_send())
    each(lambda k: q_copy(k).wait_send())
    each(lambda k: t_copy(k).wait_send())
    each(lambda k: u_copy(k).wait_send())
    each(lambda k: v_copy(k).wait_send())


def on_device(
    tokens, router_w, router_b, hidden, teacher_idx, merge_map, merge_coef, source_w, out_grad
):
    grad_scale = 1.0 / math.sqrt(TOK * 256)
    vmem = pl.BlockSpec(memory_space=pltpu.VMEM)
    smem = pl.BlockSpec(memory_space=pltpu.SMEM)
    dma = lambda n: pltpu.SemaphoreType.DMA((n,))
    rows = pltpu.VMEM((80, 8, WIDE), BF)
    mat = pltpu.VMEM((ROWS, WIDE), BF)
    share = source_w.shape[1]

    def body(*refs):
        kernel(grad_scale, *refs)

    mixed, hidden_grad, token_grad, total, small, expert_grad = pl.pallas_call(
        body,
        out_shape=(
            jax.ShapeDtypeStruct((TOK, WIDE), BF),
            jax.ShapeDtypeStruct((SLOTS, WIDE), BF),
            jax.ShapeDtypeStruct((FEAT, TOK), BF),
            jax.ShapeDtypeStruct((EXPERTS, 3072), F32),
            jax.ShapeDtypeStruct((8, 128), F32),
            jax.ShapeDtypeStruct((EXPERTS, 3, 8, 384), F32),
        ),
        in_specs=[vmem] * 7 + [smem] * 2 + [pl.BlockSpec(memory_space=pl.ANY)],
        out_specs=(vmem,) * 6,
        scratch_shapes=[
            pltpu.VMEM((EXPERTS, 3, 8, 384), BF),
            pltpu.VMEM((EXPERTS, 3, 8, 384), BF),
            pltpu.VMEM((16, 3, 8, 384), BF),
            pltpu.VMEM((ROWS, SLOTS), BF),
            mat,
            pltpu.VMEM((1, SLOTS), F32),
            pltpu.VMEM((EXPERTS, SLOTS), F32),
            rows, rows,
            pltpu.VMEM((8, 8, 3, 8, WIDE), BF),
            rows, rows, mat, mat,
            pltpu.VMEM((WIDE, WIDE), BF),
            rows, rows,
            pltpu.VMEM((8, 8, 3, 8, WIDE), BF),
            pltpu.VMEM((2, 8, 8, 3, 8, 384), BF),
            pltpu.VMEM((2, 7, 8, 3, 8, 384), BF),
            pltpu.VMEM((2, 7, 8, 3, 8, 384), BF),
            pltpu.VMEM((2, 8, 3, 8, 384), BF),
            pltpu.VMEM((16, 3, 8, 384), BF),
            pltpu.VMEM((EXPERTS, 3072), F32),
            pltpu.VMEM((16, 8, 768), F32),
            pltpu.VMEM((8, 768), F32),
            pltpu.VMEM((16, 8, 768), F32),
            pltpu.VMEM((8, 768), F32),
            pltpu.VMEM((8, 128), F32),
            pltpu.VMEM((16, 8, 128), F32),
            pltpu.VMEM((8, 128), F32),
            pltpu.VMEM((16, 8, 128), F32),
            dma(2),
            dma(16), dma(16), dma(16), dma(16), dma(16), dma(16),
            dma(4), dma(4), dma(3), dma(3), dma(8), dma(8),
            dma(16), dma(16), pltpu.SemaphoreType.DMA((2, 16)), pltpu.SemaphoreType.DMA((2, 16)),
            dma(2), dma(2),
            dma(7), dma(7), dma(7), dma(7), dma(16), dma(16),
            dma(16), dma(16), dma(16), dma(16), dma(16), dma(16),
            dma(16), dma(16), dma(16), dma(16),
        ],
        compiler_params=pltpu.CompilerParams(
            collective_id=0, has_side_effects=True, vmem_limit_bytes=67043328
        ),
        name="whole",
    )(
        tokens[0].T,
        router_w.T,
        router_b.reshape(1, EXPERTS),
        hidden.reshape(SLOTS, WIDE),
        teacher_idx[0].T,
        merge_map.reshape(1, EXPERTS),
        out_grad.reshape(TOK, WIDE),
        merge_map,
        merge_coef,
        source_w.reshape(EXPERTS, 3, 8, WIDE),
    )
    return (
        mixed.reshape(1, TOK, WIDE),
        hidden_grad.reshape(1, TOK, TOP, WIDE),
        token_grad.T[None],
        total[:, :FEAT].T,
        small[0, 32:64],
        small[0, :32],
        expert_grad.reshape(EXPERTS, share, 384),
    )


def solution(mesh):
    fine = jax.sharding.Mesh(mesh.devices.reshape(4, 2, 8, 2, 2), ("x", "yl", "z", "yh", "c"))
    ctx, rep = ("x", "yl", "z"), ("yh", "c")
    in_specs = (
        P(rep, ctx, None),
        P(),
        P(),
        P(rep, ctx, None, None),
        P(rep, ctx, None),
        P(),
        P(),
        P(None, ctx, None),
        P(rep, ctx, None),
    )
    out_specs = (
        P(rep, ctx, None),
        P(rep, ctx, None, None),
        P(rep, ctx, None),
        P(),
        P(),
        P(),
        P(None, ctx, rep),
    )
    return jax.shard_map(
        on_device, mesh=fine, in_specs=in_specs, out_specs=out_specs, check_vma=False
    )
```

time: 435 us -> 172 us (0.40)
  waiting for transfers between devices: 162 us -> 0 us
  blocking collectives: 78 us -> 0 us
  Pallas kernels: 138 us -> 157 us
  matrix products: 16.6 us -> 0 us
  between operations: 14.3 us -> 0.65 us
  other arithmetic: 8.25 us -> 0 us
    psum x1 -> x0, waiting for transfers between devices: 162 us -> none  [on_device(): sum_w, sum_b, sum_c = lax.psum((part_w, part_b, part_c), every)]
    psum x1 -> x0, blocking collectives: 78 us -> none  [on_device(): sum_w, sum_b, sum_c = lax.psum((part_w, part_b, part_c), every)]
    pallas_call x1, Pallas kernels: 138 us -> 157 us  [on_device(): pl.pallas_call(body, out_shape=(jax.ShapeDtypeStruct((TOK, WIDE), BF), ja...]
    dot_general x8 -> x0, matrix products: 16.6 us -> none  [the longest x1 4.05 us: on_device(): slot_out = jnp.dot(spread, home_out, preferred_element_type=jnp.float32)]
    mul x2 -> x0, local copies, waits for them, and re-layouts: 7.05 us -> none  [on_device(): gate[:, :, None] * og[:, None, :]]
    mul x6 -> x0, other arithmetic: 5.24 us -> none  [the longest x2 2.44 us: on_device(): source_w_grad = source_grad * (merge_coef * grad_scale)[:, None, None]]
  transfers between devices with their start and end apart: 1 -> 0, of which waited for: 1 -> 0; matrix products, arithmetic and copies ran while one was open for 2% -> 0% of each run, Pallas kernels for 0% -> 0%
where the time goes in v4:
time: 172 us; the launch traced here: 171 us
  Pallas kernels  157 us (91%)
  local copies, waits for them, and re-layouts  13.4 us (8%)
    pallas_call x1, Pallas kernels, on_device(): pl.pallas_call(body, out_shape=(jax.ShapeDtypeStruct((TOK, WIDE), BF), ja...  157 us
    reshape x1, local copies, waits for them, and re-layouts, on_device(): hidden_grad.reshape(1, TOK, TOP, WIDE)  3.94 us
    reshape x1, local copies, waits for them, and re-layouts, on_device(): hidden.reshape(SLOTS, WIDE)  3.71 us

profile of v4, /device:TPU:1, one launch (start us, length us, event | category | flops | bytes accessed | tf_op | source)
XLA Modules:
  0.0 171.3 jit_solution(13035339714363007165)
XLA Ops:
  0.6 3.7 %reshape.39.refs_3_ = bf16[512,1536]{1,0:T(8,128)(2,1)} reshape(bf16[1,128,4,1536]{3,2,1,0:T(4,128)(2,1)} %param.12) | data formatting | bytes 3145728 | tf_op jit(solution)/shard_map/reshape | solution.py:566
  4.3 157.3 %whole.1 = (bf16[128,1536]{1,0:T(8,128)(2,1)}, bf16[512,1536]{1,0:T(8,128)(2,1)}, bf16[2880,128]{1,0:T(8,128)(2,1)}, f32[32,3072]{1,0:T(8,128)}, f32[8,128]{1,0:T(8,128)}, /*index=5*/f32[32,3,8,384]{3,2,1,0:T(8,128)}) custom-call(bf16[2880,128]{1,0:T(8,128)(2,1)} %bitcast.24, bf16[32,2880]{1,0:T(8,128)(2,1)} %bitcast.28, f32[1,32]{1,0:T(1,128)} %bitcast.31, ...), custom_call_target="tpu_custom_call" | custom-call | tf_op jit(solution)/shard_map/whole/pallas_call | solution.py:509
  161.7 1.3 slice_bitcast_fusion.1
  163.0 1.8 %slice_bitcast_fusion = f32[2880,32]{0,1:T(8,128)} fusion(f32[32,3072]{1,0:T(8,128)} %get-tuple-element.16), kind=kLoop, calls=%fused_computation | loop fusion | bytes 737280 | tf_op jit(solution)/shard_map/transpose | solution.py:578
  164.8 0.0 copy-start.2
  164.8 0.0 copy-start.1
  164.8 3.9 %reshape.44 = bf16[1,128,4,1536]{3,2,1,0:T(4,128)(2,1)} reshape(bf16[512,1536]{1,0:T(8,128)(2,1)} %get-tuple-element.14) | data formatting | bytes 3145728 | tf_op jit(solution)/shard_map/reshape | solution.py:576
  168.7 0.0 copy-done.2
  168.7 0.0 copy-start
  168.7 0.7 copy.19
  169.5 0.0 copy-done.1
  169.5 0.9 copy.20
  170.3 0.0 copy-done
  170.3 1.0 copy.21
Async XLA Ops:
  164.8 3.9 %copy-start.2 = (bf16[128,1536]{1,0:T(8,128)(2,1)S(1)}, bf16[128,1536]{1,0:T(8,128)(2,1)}, u32[]{:S(2)}) copy-start(bf16[128,1536]{1,0:T(8,128)(2,1)} %get-tuple-element.13) | copy-start | bytes 1179652
  164.8 4.7 %copy-start.1 = (bf16[2880,128]{1,0:T(8,128)(2,1)S(1)}, bf16[2880,128]{1,0:T(8,128)(2,1)}, u32[]{:S(2)}) copy-start(bf16[2880,128]{1,0:T(8,128)(2,1)} %get-tuple-element.15) | copy-start | bytes 2211844
  168.7 1.6 copy-start

commit v5 on v4

--- a/solution.py
+++ b/solution.py
@@ -75,12 +75,13 @@
     src_a, src_b, wq, sel, og_rows, gate_s, pick_s, send_h, send_g,
     weight, recv_h, recv_g, mat_h, mat_g, mat_w, home_out, home_back,
     part, sib, ring_send, ring_recv, last, got,
-    table, first, mine, second, done, row_a, row_b, row_c, row_d,
+    table, first, mine, second, done, row_a, row_b, row_c, row_d, prods,
     l_sem,
-    a_s, a_r, h_s, h_r, g_s, g_r, zp_s, zp_r, zm_s, zm_r, w_s, w_r,
-    o_s, o_r, b_s, b_r, e_s, e_r, rp_s, rp_r, rm_s, rm_r, l_s, l_r,
+    a_s, a_r, zp_s, zp_r, zm_s, zm_r, w_s, w_r, e_s, e_r, rp_s, rp_r, rm_s, rm_r, l_s, l_r,
     p_s, p_r, q_s, q_r, t_s, t_r, u_s, u_r, v_s, v_r,
+    relay_h, relay_g, relay_o, relay_b, *sems,
 ):
+    sem_h, sem_g, sem_o, sem_b = sems[:4], sems[4:8], sems[8:12], sems[12:]
     x, yl, z = lax.axis_index("x"), lax.axis_index("yl"), lax.axis_index("z")
     yh, c = lax.axis_index("yh"), lax.axis_index("c")
     y = yh * 2 + yl
@@ -135,10 +136,18 @@
     sel[...] = (iota((ROWS, SLOTS), 0) == index_row).astype(F32).astype(BF)
     pick_s[...] = pick.astype(F32)
 
+    def slot_rows(i, carry):
+        mat_g[pl.ds(pl.multiple_of(i * 64, 64), 64), :] = (
+            hid[pl.ds(i * 16, 16)].astype(F32).reshape(64, WIDE).astype(BF)
+        )
+        return carry
+
+    lax.fori_loop(0, 8, slot_rows, 0)
+
     def pack_h(j, carry):
         span = pl.ds(pl.multiple_of(j * 256, 256), 256)
-        tile = jnp.dot(sel[...], hid[:, span], preferred_element_type=F32)
-        send_h[:, :, span] = tile.reshape(80, 8, 256).astype(BF)
+        tile = jnp.dot(sel[...], mat_g[pl.ds(0, SLOTS), span], preferred_element_type=F32)
+        send_h[:, :, :, :, span] = tile.reshape(4, 4, 5, 8, 256).astype(BF)
         return carry
 
     lax.fori_loop(0, 6, pack_h, 0)
@@ -160,12 +169,75 @@
     lax.fori_loop(0, 16, merge, 0)
     pl.semaphore_wait(barrier, 30)
 
-    def plane_copy(k, src, dst, send, recv):
-        px, py = offset(k, x, y)
-        return remote(
-            src.at[pl.ds(5 * (px * 4 + py), 5)], dst.at[pl.ds(5 * me, 5)],
-            send.at[k], recv.at[k], plane_id(px, py),
-        )
+    low_cols, high_cols = pl.ds(0, 768), pl.ds(768, 768)
+
+    class Shuffle:
+        def __init__(self, src, dst, relay, s1, r1, s2, r2):
+            self.src, self.dst, self.relay = src, dst, relay
+            self.s1, self.r1, self.s2, self.r2 = s1, r1, s2, r2
+
+        def first(self, f, d):
+            if f == 0:
+                px = lax.rem(x + d, 4)
+                src, where = self.src.at[px, :, :, :, low_cols], plane_id(px, y)
+            else:
+                py = lax.rem(y + d, 4)
+                src, where = self.src.at[:, py, :, :, high_cols], plane_id(x, py)
+            return remote(
+                src, self.relay.at[f, d - 1], self.s1.at[f, d - 1], self.r1.at[f, d - 1], where
+            )
+
+        def second(self, f, d, e):
+            if f == 0:
+                py, px = lax.rem(y + e, 4), lax.rem(x + 4 - d, 4)
+                src = (
+                    self.src.at[x, py, :, :, low_cols] if d == 0 else self.relay.at[0, d - 1, py]
+                )
+                dst, where = self.dst.at[px, y, :, :, low_cols], plane_id(x, py)
+            else:
+                px, py = lax.rem(x + e, 4), lax.rem(y + 4 - d, 4)
+                src = (
+                    self.src.at[px, y, :, :, high_cols] if d == 0 else self.relay.at[1, d - 1, px]
+                )
+                dst, where = self.dst.at[x, py, :, :, high_cols], plane_id(px, y)
+            return remote(src, dst, self.s2.at[f, d, e - 1], self.r2.at[f, d, e - 1], where)
+
+        def start(self):
+            for d in (1, 3, 2):
+                for f in range(2):
+                    self.first(f, d).start()
+            for e in (1, 3, 2):
+                for f in range(2):
+                    self.second(f, 0, e).start()
+            self.dst[x, y] = self.src[x, y]
+
+        def forward(self, d):
+            for f in range(2):
+                self.first(f, d).wait_recv()
+                for e in (1, 3, 2):
+                    self.second(f, d, e).start()
+            px, py = lax.rem(x + 4 - d, 4), lax.rem(y + 4 - d, 4)
+            self.dst[px, y, :, :, low_cols] = self.relay[0, d - 1, y]
+            self.dst[x, py, :, :, high_cols] = self.relay[1, d - 1, x]
+
+        def arrive(self):
+            for f in range(2):
+                for d in range(4):
+                    for e in range(1, 4):
+                        self.second(f, d, e).wait_recv()
+
+        def drain(self):
+            for f in range(2):
+                for d in range(1, 4):
+                    self.first(f, d).wait_send()
+                for d in range(4):
+                    for e in range(1, 4):
+                        self.second(f, d, e).wait_send()
+
+    move_h = Shuffle(send_h, recv_h, relay_h, *sem_h)
+    move_g = Shuffle(send_g, recv_g, relay_g, *sem_g)
+    move_o = Shuffle(send_h, home_out, relay_o, *sem_o)
+    move_b = Shuffle(send_g, home_back, relay_b, *sem_b)
 
     def a_copy(k):
         px, py = offset(k, x, y)
@@ -174,24 +246,6 @@
             plane_id(px, py),
         )
 
-    def h_copy(k):
-        return plane_copy(k, send_h, recv_h, h_s, h_r)
-
-    def g_copy(k):
-        return plane_copy(k, send_g, recv_g, g_s, g_r)
-
-    def o_copy(k):
-        return plane_copy(k, send_h, home_out, o_s, o_r)
-
-    def b_copy(k, n):
-        px, py = offset(k, x, y)
-        cols = pl.ds(n * 768, 768)
-        return remote(
-            send_g.at[pl.ds(5 * (px * 4 + py), 5), :, cols],
-            home_back.at[pl.ds(5 * me, 5), :, cols],
-            b_s.at[n, k], b_r.at[n, k], plane_id(px, py),
-        )
-
     def l_copy(k):
         px, py = offset(k, x, y)
         return remote(
@@ -200,10 +254,8 @@
         )
 
     each(lambda k: a_copy(k).start())
-    each(lambda k: h_copy(k).start())
-    own = pl.ds(5 * me, 5)
+    move_h.start()
     weight[xy, z, :, :, quarter] = wq[me]
-    recv_h[own] = send_h[own]
 
     logits = jnp.dot(
         router_t[...], tokens[...], preferred_element_type=F32
@@ -219,9 +271,8 @@
         span = pl.ds(j * 256, 256)
         tile = jnp.dot(row_token, og[:, span], preferred_element_type=F32)
         og_rows[:, span] = tile.astype(BF)
-        send_g[:, :, span] = (tile * gate_col).reshape(80, 8, 256).astype(BF)
-    each(lambda k: g_copy(k).start())
-    recv_g[own] = send_g[own]
+        send_g[:, :, :, :, span] = (tile * gate_col).reshape(4, 4, 5, 8, 256).astype(BF)
+    move_g.start()
 
     each(lambda k: a_copy(k).wait_recv())
 
@@ -244,6 +295,15 @@
     zm_copy(0).start()
     w_copy(0).start()
     for s in range(4):
+        if s == 0:
+            move_h.forward(1)
+            move_h.forward(3)
+        elif s == 1:
+            move_h.forward(2)
+        elif s == 2:
+            move_g.forward(1)
+        else:
+            move_g.forward(3)
         zp_copy(s).wait_recv()
         if s < 3:
             zp_copy(s + 1).start()
@@ -257,13 +317,14 @@
     def reshape_rows(src, dst):
         def step(i, carry):
             dst[pl.ds(pl.multiple_of(i * 80, 80), 80), :] = (
-                src[pl.ds(i * 10, 10)].astype(F32).reshape(80, WIDE).astype(BF)
+                src[i // 2, pl.ds(lax.rem(i, 2) * 2, 2)].astype(F32).reshape(80, WIDE).astype(BF)
             )
             return carry
 
         lax.fori_loop(0, 8, step, 0)
 
-    each(lambda k: h_copy(k).wait_recv())
+    move_g.forward(2)
+    move_h.arrive()
     reshape_rows(recv_h, mat_h)
     for i in range(8):
         w_copy(i).wait_recv()
@@ -275,20 +336,19 @@
         return carry
 
     lax.fori_loop(0, 8, shape_w, 0)
-    each(lambda k: h_copy(k).wait_send())
+    move_h.drain()
 
     def forward(j, carry):
         span = pl.ds(pl.multiple_of(j * 256, 256), 256)
         tile = lax.dot_general(
             mat_h[...], mat_w[span, :], (((1,), (1,)), ((), ())), preferred_element_type=F32
         )
-        send_h[:, :, span] = tile.reshape(80, 8, 256).astype(BF)
+        send_h[:, :, :, :, span] = tile.reshape(4, 4, 5, 8, 256).astype(BF)
         return carry
 
     lax.fori_loop(0, 6, forward, 0)
-    each(lambda k: o_copy(k).start())
-    home_out[own] = send_h[own]
-    each(lambda k: g_copy(k).wait_recv())
+    move_o.start()
+    move_g.arrive()
     reshape_rows(recv_g, mat_g)
 
     def outer(i, carry):
@@ -309,12 +369,12 @@
 
     for h in range(2):
         e_copy(h).start()
-    each(lambda k: g_copy(k).wait_send())
+    move_g.drain()
 
     def backward(j, carry):
         span = pl.ds(pl.multiple_of(j * 256, 256), 256)
         tile = jnp.dot(mat_g[...], mat_w[:, span], preferred_element_type=F32)
-        send_g[:, :, span] = tile.reshape(80, 8, 256).astype(BF)
+        send_g[:, :, :, :, span] = tile.reshape(4, 4, 5, 8, 256).astype(BF)
         return carry
 
     def local(h, b):
@@ -340,29 +400,28 @@
             ring_send[h, s] = value.astype(BF)
             ring(h, s).start()
 
+    move_o.forward(1)
     lax.fori_loop(0, 3, backward, 0)
-    each(lambda k: b_copy(k, 0).start())
+    move_o.forward(3)
+    lax.fori_loop(3, 6, backward, 0)
+    move_b.start()
     for h in range(2):
         e_copy(h).wait_recv()
     ring_step(0)
-    lax.fori_loop(3, 6, backward, 0)
-    each(lambda k: b_copy(k, 1).start())
-    home_back[own] = send_g[own]
-    for s in range(1, 7):
-        ring_step(s)
-    load_b.wait()
-    for h in range(2):
-        value = local(h, z)
-        ring(h, 6).wait_recv()
-        last[h] = (value + ring_recv[h, 6].astype(F32)).astype(BF)
-    each(lambda k: l_copy(k).start())
-    got[me] = last[yh, xy]
-
-    each(lambda k: o_copy(k).wait_recv())
+    move_o.forward(2)
+    ring_step(1)
+    ring_step(2)
+    move_b.forward(1)
+    ring_step(3)
+    move_b.forward(3)
+    ring_step(4)
+    move_b.forward(2)
+
+    move_o.arrive()
 
     def score_rows(i, carry):
         rows = pl.ds(pl.multiple_of(i * 80, 80), 80)
-        value = home_out[pl.ds(i * 10, 10)].astype(F32).reshape(80, WIDE)
+        value = home_out[i // 2, pl.ds(lax.rem(i, 2) * 2, 2)].astype(F32).reshape(80, WIDE)
         mat_h[rows, :] = value.astype(BF)
         score = jnp.sum(value * og_rows[rows, :].astype(F32), axis=1, keepdims=True)
         return carry + jnp.sum(
@@ -398,35 +457,51 @@
 
     each(lambda k: p_copy(k).start())
     first[me] = table[spot(x, y)]
-    each(lambda k: l_copy(k).wait_recv())
-
-    def coefficient(e, carry):
-        grad = got[map_s[e]].astype(F32)
-        prod = jnp.sum(jnp.sum(grad * src_b[e].astype(F32), axis=0), axis=0, keepdims=True)
-        dot = jnp.sum(prod, axis=1, keepdims=True)
-        return carry + jnp.where(iota((1, 128), 1) == e, dot, 0.0)
-
-    coef_row = lax.fori_loop(0, EXPERTS, coefficient, jnp.zeros((1, 128), F32))
-    bias_row = jnp.sum(
-        jnp.where(iota((EXPERTS, 128), 1) - 32 == iota((EXPERTS, 128), 0), bias_col, 0.0),
-        axis=0, keepdims=True,
-    )
-    row_a[...] = jnp.broadcast_to(coef_row + bias_row, (8, 128))
-
-    def u_copy(k):
-        px, py = offset(k, x, y)
-        return remote(row_a, row_b.at[me], u_s.at[k], u_r.at[k], plane_id(px, py))
-
-    def v_copy(k):
-        return remote(row_c, row_d.at[zc], v_s.at[k], v_r.at[k], line(k))
-
-    each(lambda k: u_copy(k).start())
-    row_b[me] = row_a[...]
+    for s in range(5, 7):
+        ring_step(s)
+    load_b.wait()
+    for h in range(2):
+        value = local(h, z)
+        ring(h, 6).wait_recv()
+        last[h] = (value + ring_recv[h, 6].astype(F32)).astype(BF)
+    each(lambda k: l_copy(k).start())
+    got[me] = last[yh, xy]
 
     each(lambda k: p_copy(k).wait_recv())
     mine[...] = jnp.sum(first[...], axis=0)
     each(lambda k: q_copy(k).start())
     second[zc] = mine[...]
+    each(lambda k: l_copy(k).wait_recv())
+
+    def coefficient(e, carry):
+        prod = jnp.sum(got[map_s[e]].astype(F32) * src_b[e].astype(F32), axis=0)
+        prods[e] = prod[:, :128] + prod[:, 128:256] + prod[:, 256:]
+        return carry
+
+    lax.fori_loop(0, EXPERTS, coefficient, 0)
+    dots = jnp.sum(jnp.sum(prods[...], axis=1), axis=1, keepdims=True)
+    at = iota((EXPERTS, 128), 1) == iota((EXPERTS, 128), 0)
+    coef_row = jnp.sum(jnp.where(at, dots, 0.0), axis=0, keepdims=True)
+    bias_row = jnp.sum(
+        jnp.where(iota((EXPERTS, 128), 1) - 32 == iota((EXPERTS, 128), 0), bias_col, 0.0),
+        axis=0, keepdims=True,
+    )
+    row_a[...] = jnp.broadcast_to(coef_row + bias_row, (8, 128))
+
+    def u_copy(k):
+        px, py = offset(k, x, y)
+        return remote(row_a, row_b.at[me], u_s.at[k], u_r.at[k], plane_id(px, py))
+
+    def v_copy(k):
+        return remote(row_c, row_d.at[zc], v_s.at[k], v_r.at[k], line(k))
+
+    each(lambda k: u_copy(k).start())
+    row_b[me] = row_a[...]
+
+    each(lambda k: q_copy(k).wait_recv())
+    done[...] = jnp.sum(second[...], axis=0) * grad_scale
+    each(lambda k: t_copy(k).start())
+    total[spot(x, y)] = done[...]
 
     def expert(e, carry):
         expert_grad[e] = got[map_s[e]].astype(F32) * (coef_s[e] * grad_scale)
@@ -440,10 +515,6 @@
     token_grad[...] = lax.dot_general(
         router_t[...], logit_half, (((0,), (0,)), ((), ())), preferred_element_type=F32
     ).astype(BF)
-    each(lambda k: q_copy(k).wait_recv())
-    done[...] = jnp.sum(second[...], axis=0) * grad_scale
-    each(lambda k: t_copy(k).start())
-    total[spot(x, y)] = done[...]
     slot_token = iota((TOK, SLOTS), 1) // TOP == iota((TOK, SLOTS), 0)
     spread_gate = jnp.where(slot_token, gate, 0.0)
     high = spread_gate.astype(BF)
@@ -458,14 +529,14 @@
         jnp.dot(over_rows(high), mat_h[...], preferred_element_type=F32)
         + jnp.dot(over_rows(low), mat_h[...], preferred_element_type=F32)
     ).astype(BF)
-    for n in range(2):
-        each(lambda k: b_copy(k, n).wait_recv())
+    move_b.arrive()
     reshape_rows(home_back, mat_g)
     for j in range(6):
         span = pl.ds(j * 256, 256)
-        hidden_grad[:, span] = lax.dot_general(
+        tile = lax.dot_general(
             sel[...], mat_g[:, span], (((0,), (0,)), ((), ())), preferred_element_type=F32
-        ).astype(BF)
+        )
+        hidden_grad[:, :, span] = tile.reshape(TOK, TOP, 256).astype(BF)
     each(lambda k: v_copy(k).wait_recv())
     small[...] = jnp.sum(row_d[...], axis=0) * grad_scale
     each(lambda k: t_copy(k).wait_recv())
@@ -481,9 +552,8 @@
         e_copy(h).wait_send()
         for s in range(7):
             ring(h, s).wait_send()
-    each(lambda k: o_copy(k).wait_send())
-    for n in range(2):
-        each(lambda k: b_copy(k, n).wait_send())
+    move_o.drain()
+    move_b.drain()
     each(lambda k: l_copy(k).wait_send())
     each(lambda k: p_copy(k).wait_send())
     each(lambda k: q_copy(k).wait_send())
@@ -499,7 +569,10 @@
     vmem = pl.BlockSpec(memory_space=pltpu.VMEM)
     smem = pl.BlockSpec(memory_space=pltpu.SMEM)
     dma = lambda n: pltpu.SemaphoreType.DMA((n,))
-    rows = pltpu.VMEM((80, 8, WIDE), BF)
+    rows = pltpu.VMEM((4, 4, 5, 8, WIDE), BF)
+    relay = pltpu.VMEM((2, 3, 4, 5, 8, 768), BF)
+    one = pltpu.SemaphoreType.DMA((2, 3))
+    two = pltpu.SemaphoreType.DMA((2, 4, 3))
     mat = pltpu.VMEM((ROWS, WIDE), BF)
     share = source_w.shape[1]
 
@@ -510,7 +583,7 @@
         body,
         out_shape=(
             jax.ShapeDtypeStruct((TOK, WIDE), BF),
-            jax.ShapeDtypeStruct((SLOTS, WIDE), BF),
+            jax.ShapeDtypeStruct((TOK, TOP, WIDE), BF),
             jax.ShapeDtypeStruct((FEAT, TOK), BF),
             jax.ShapeDtypeStruct((EXPERTS, 3072), F32),
             jax.ShapeDtypeStruct((8, 128), F32),
@@ -546,15 +619,16 @@
             pltpu.VMEM((16, 8, 128), F32),
             pltpu.VMEM((8, 128), F32),
             pltpu.VMEM((16, 8, 128), F32),
+            pltpu.VMEM((EXPERTS, 8, 128), F32),
             dma(2),
-            dma(16), dma(16), dma(16), dma(16), dma(16), dma(16),
-            dma(4), dma(4), dma(3), dma(3), dma(8), dma(8),
-            dma(16), dma(16), pltpu.SemaphoreType.DMA((2, 16)), pltpu.SemaphoreType.DMA((2, 16)),
+            dma(16), dma(16), dma(4), dma(4), dma(3), dma(3), dma(8), dma(8),
             dma(2), dma(2),
             dma(7), dma(7), dma(7), dma(7), dma(16), dma(16),
             dma(16), dma(16), dma(16), dma(16), dma(16), dma(16),
             dma(16), dma(16), dma(16), dma(16),
-        ],
+            relay, relay, relay, relay,
+        ]
+        + [one, one, two, two] * 4,
         compiler_params=pltpu.CompilerParams(
             collective_id=0, has_side_effects=True, vmem_limit_bytes=67043328
         ),
@@ -563,7 +637,7 @@
         tokens[0].T,
         router_w.T,
         router_b.reshape(1, EXPERTS),
-        hidden.reshape(SLOTS, WIDE),
+        hidden[0],
         teacher_idx[0].T,
         merge_map.reshape(1, EXPERTS),
         out_grad.reshape(TOK, WIDE),
@@ -573,7 +647,7 @@
     )
     return (
         mixed.reshape(1, TOK, WIDE),
-        hidden_grad.reshape(1, TOK, TOP, WIDE),
+        hidden_grad[None],
         token_grad.T[None],
         total[:, :FEAT].T,
         small[0, 32:64],

time: 172 us -> 153 us (0.89)
  Pallas kernels: 157 us -> 143 us
  local copies, waits for them, and re-layouts: 13.4 us -> 9.96 us
    pallas_call x1, Pallas kernels: 157 us -> 143 us  [on_device(): pl.pallas_call(body, out_shape=(jax.ShapeDtypeStruct((TOK, WIDE), BF), ja...]
    reshape x2 -> x0, local copies, waits for them, and re-layouts: 7.65 us -> none  [the longest x1 3.94 us: on_device(): hidden_grad.reshape(1, TOK, TOP, WIDE)]
    unnamed x9 -> x8, local copies, waits for them, and re-layouts: 2.63 us -> 6.88 us
where the time goes in v5:
time: 153 us
  Pallas kernels  143 us (93%)
  local copies, waits for them, and re-layouts  9.96 us (7%)
    pallas_call x1, Pallas kernels, on_device(): pl.pallas_call(body, out_shape=(jax.ShapeDtypeStruct((TOK, WIDE), BF), ja...  143 us
    unnamed x8, local copies, waits for them, and re-layouts  6.88 us

profile of v5, /device:TPU:1, one launch (start us, length us, event | category | flops | bytes accessed | tf_op | source)
XLA Modules:
  0.0 153.2 jit_solution(12925528747198991840)
XLA Ops:
  0.6 142.6 %whole.1 = (bf16[128,1536]{1,0:T(8,128)(2,1)}, bf16[128,4,1536]{2,1,0:T(4,128)(2,1)}, bf16[2880,128]{1,0:T(8,128)(2,1)}, f32[32,3072]{1,0:T(8,128)}, f32[8,128]{1,0:T(8,128)}, /*index=5*/f32[32,3,8,384]{3,2,1,0:T(8,128)}) custom-call(bf16[2880,128]{1,0:T(8,128)(2,1)} %bitcast.28, bf16[32,2880]{1,0:T(8,128)(2,1)} %bitcast.32, f32[1,32]{1,0:T(1,128)} %bitcast.35, ...), custom_call_target="tpu_custom_call" | custom-call | tf_op jit(solution)/shard_map/whole/pallas_call | solution.py:582
  143.2 1.3 slice_bitcast_fusion.1
  144.5 1.8 %slice_bitcast_fusion = f32[2880,32]{0,1:T(8,128)} fusion(f32[32,3072]{1,0:T(8,128)} %get-tuple-element.16), kind=kLoop, calls=%fused_computation | loop fusion | bytes 737280 | tf_op jit(solution)/shard_map/transpose | solution.py:652
  146.3 1.8 %copy.20 = bf16[1,128,1536]{2,1,0:T(8,128)(2,1)} copy(bf16[1,128,1536]{2,1,0:T(8,128)(2,1)} %bitcast.31) | data formatting | bytes 786432
  148.0 0.0 copy-start.1
  148.1 0.0 copy-start
  148.1 3.2 %copy.21 = bf16[1,128,4,1536]{3,2,1,0:T(4,128)(2,1)} copy(bf16[1,128,4,1536]{3,2,1,0:T(4,128)(2,1)} %bitcast.25) | data formatting | bytes 3145728
  151.3 0.0 copy-done.1
  151.3 0.9 copy.22
  152.1 0.0 copy-done
  152.2 1.0 copy.23
Async XLA Ops:
  148.0 3.2 %copy-start.1 = (bf16[2880,128]{1,0:T(8,128)(2,1)S(1)}, bf16[2880,128]{1,0:T(8,128)(2,1)}, u32[]{:S(2)}) copy-start(bf16[2880,128]{1,0:T(8,128)(2,1)} %get-tuple-element.15) | copy-start | bytes 2211844
  148.1 4.1 %copy-start = (f32[32,3,8,384]{3,2,1,0:T(8,128)S(1)}, f32[32,3,8,384]{3,2,1,0:T(8,128)}, u32[]{:S(2)}) copy-start(f32[32,3,8,384]{3,2,1,0:T(8,128)} %get-tuple-element.18) | copy-start | bytes 3538948

commit v6 on v5

--- a/solution.py
+++ b/solution.py
@@ -377,28 +377,35 @@
         send_g[:, :, :, :, span] = tile.reshape(4, 4, 5, 8, 256).astype(BF)
         return carry
 
-    def local(h, b):
+    def local(h, b, n):
         here = pl.ds(pl.multiple_of(h * 768 + c * 384, 384), 384)
-        return part[:, b, :, :, here].astype(F32) + sib[h, :, b].astype(F32)
-
-    def ring(h, s):
+        return part[pl.ds(4 * n, 4), b, :, :, here].astype(F32) + sib[
+            h, pl.ds(4 * n, 4), b
+        ].astype(F32)
+
+    def ring(h, s, n):
+        some = pl.ds(4 * n, 4)
         if h == 0:
             return remote(
-                ring_send.at[0, s], ring_recv.at[0, s], rp_s.at[s], rp_r.at[s], {"z": up}
+                ring_send.at[0, s, some], ring_recv.at[0, s, some],
+                rp_s.at[n, s], rp_r.at[n, s], {"z": up},
             )
         return remote(
-            ring_send.at[1, s], ring_recv.at[1, s], rm_s.at[s], rm_r.at[s], {"z": down}
+            ring_send.at[1, s, some], ring_recv.at[1, s, some],
+            rm_s.at[n, s], rm_r.at[n, s], {"z": down},
         )
 
     def ring_step(s):
-        for h in range(2):
-            b = lax.rem(z + 15 - s, 8) if h == 0 else lax.rem(z + 1 + s, 8)
-            value = local(h, b)
-            if s > 0:
-                ring(h, s - 1).wait_recv()
-                value = value + ring_recv[h, s - 1].astype(F32)
-            ring_send[h, s] = value.astype(BF)
-            ring(h, s).start()
+        for n in range(2):
+            for h in range(2):
+                some = pl.ds(4 * n, 4)
+                b = lax.rem(z + 15 - s, 8) if h == 0 else lax.rem(z + 1 + s, 8)
+                value = local(h, b, n)
+                if s > 0:
+                    ring(h, s - 1, n).wait_recv()
+                    value = value + ring_recv[h, s - 1, some].astype(F32)
+                ring_send[h, s, some] = value.astype(BF)
+                ring(h, s, n).start()
 
     move_o.forward(1)
     lax.fori_loop(0, 3, backward, 0)
@@ -460,10 +467,12 @@
     for s in range(5, 7):
         ring_step(s)
     load_b.wait()
-    for h in range(2):
-        value = local(h, z)
-        ring(h, 6).wait_recv()
-        last[h] = (value + ring_recv[h, 6].astype(F32)).astype(BF)
+    for n in range(2):
+        for h in range(2):
+            some = pl.ds(4 * n, 4)
+            value = local(h, z, n)
+            ring(h, 6, n).wait_recv()
+            last[h, some] = (value + ring_recv[h, 6, some].astype(F32)).astype(BF)
     each(lambda k: l_copy(k).start())
     got[me] = last[yh, xy]
 
@@ -551,7 +560,8 @@
     for h in range(2):
         e_copy(h).wait_send()
         for s in range(7):
-            ring(h, s).wait_send()
+            for n in range(2):
+                ring(h, s, n).wait_send()
     move_o.drain()
     move_b.drain()
     each(lambda k: l_copy(k).wait_send())
@@ -560,6 +570,43 @@
     each(lambda k: t_copy(k).wait_send())
     each(lambda k: u_copy(k).wait_send())
     each(lambda k: v_copy(k).wait_send())
+
+
+def finish_kernel(
+    mixed, hidden_grad, token_grad, expert_grad, total, small,
+    mixed_out, hidden_out, token_out, expert_out, router_out, bias_out, coef_out, sems,
+):
+    pairs = (
+        (hidden_grad, hidden_out), (expert_grad, expert_out), (token_grad, token_out),
+        (mixed, mixed_out),
+    )
+    copies = [pltpu.make_async_copy(a, b, sems.at[i]) for i, (a, b) in enumerate(pairs)]
+    for copy in copies:
+        copy.start()
+    router_out[...] = total[:, pl.ds(0, FEAT)]
+    row = small[pl.ds(0, 1), :]
+    coef_out[...] = row[:, :EXPERTS]
+    bias_out[...] = row[:, EXPERTS : 2 * EXPERTS]
+    for copy in copies:
+        copy.wait()
+
+
+def finish(mixed, hidden_grad, token_grad, expert_grad, total, small):
+    vmem = pl.BlockSpec(memory_space=pltpu.VMEM)
+    hbm = pl.BlockSpec(memory_space=pl.ANY)
+    like = lambda v: jax.ShapeDtypeStruct(v.shape, v.dtype)
+    line = jax.ShapeDtypeStruct((1, EXPERTS), F32)
+    return pl.pallas_call(
+        finish_kernel,
+        out_shape=(
+            like(mixed), like(hidden_grad), like(token_grad), like(expert_grad),
+            jax.ShapeDtypeStruct((EXPERTS, FEAT), F32), line, line,
+        ),
+        in_specs=[hbm] * 4 + [vmem] * 2,
+        out_specs=(vmem,) * 7,
+        scratch_shapes=[pltpu.SemaphoreType.DMA((4,))],
+        name="finish",
+    )(mixed, hidden_grad, token_grad, expert_grad, total, small)
 
 
 def on_device(
@@ -572,6 +619,7 @@
     rows = pltpu.VMEM((4, 4, 5, 8, WIDE), BF)
     relay = pltpu.VMEM((2, 3, 4, 5, 8, 768), BF)
     one = pltpu.SemaphoreType.DMA((2, 3))
+    lap = pltpu.SemaphoreType.DMA((2, 7))
     two = pltpu.SemaphoreType.DMA((2, 4, 3))
     mat = pltpu.VMEM((ROWS, WIDE), BF)
     share = source_w.shape[1]
@@ -623,7 +671,7 @@
             dma(2),
             dma(16), dma(16), dma(4), dma(4), dma(3), dma(3), dma(8), dma(8),
             dma(2), dma(2),
-            dma(7), dma(7), dma(7), dma(7), dma(16), dma(16),
+            lap, lap, lap, lap, dma(16), dma(16),
             dma(16), dma(16), dma(16), dma(16), dma(16), dma(16),
             dma(16), dma(16), dma(16), dma(16),
             relay, relay, relay, relay,
@@ -645,13 +693,16 @@
         merge_coef,
         source_w.reshape(EXPERTS, 3, 8, WIDE),
     )
+    mixed, hidden_grad, token_grad, expert_grad, router, bias, coef = finish(
+        mixed, hidden_grad, token_grad, expert_grad, total, small
+    )
     return (
         mixed.reshape(1, TOK, WIDE),
         hidden_grad[None],
         token_grad.T[None],
-        total[:, :FEAT].T,
-        small[0, 32:64],
-        small[0, :32],
+        router.T,
+        bias[0],
+        coef[0],
         expert_grad.reshape(EXPERTS, share, 384),
     )
 

time: 153 us -> 143 us (0.935); the launches traced: 153 us -> 142 us
  local copies, waits for them, and re-layouts: 9.96 us -> 0 us
  Pallas kernels: 143 us -> 141 us
    unnamed x8 -> x0, local copies, waits for them, and re-layouts: 6.88 us -> none
    pallas_call x1, Pallas kernels: 143 us -> 136 us  [on_device(): pl.pallas_call(body, out_shape=(jax.ShapeDtypeStruct((TOK, WIDE), BF), ja...]
    pallas_call x0 -> x1, Pallas kernels: none -> 5.11 us  [finish(): pl.pallas_call(finish_kernel, out_shape=(like(mixed), like(hidden_grad),...]
    transpose x1 -> x0, local copies, waits for them, and re-layouts: 1.75 us -> none  [on_device(): total[:, :FEAT]]
where the time goes in v6:
time: 143 us; the launch traced here: 142 us
  Pallas kernels  141 us (99%)
    pallas_call x1, Pallas kernels, on_device(): pl.pallas_call(body, out_shape=(jax.ShapeDtypeStruct((TOK, WIDE), BF), ja...  136 us
    pallas_call x1, Pallas kernels, finish(): pl.pallas_call(finish_kernel, out_shape=(like(mixed), like(hidden_grad),...  5.11 us

profile of v6, /device:TPU:1, one launch (start us, length us, event | category | flops | bytes accessed | tf_op | source)
XLA Modules:
  0.0 141.5 jit_solution(750738446618134849)
XLA Ops:
  0.6 135.8 %whole.1 = (bf16[128,1536]{1,0:T(8,128)(2,1)}, bf16[128,4,1536]{2,1,0:T(4,128)(2,1)}, bf16[2880,128]{1,0:T(8,128)(2,1)}, f32[32,3072]{1,0:T(8,128)}, f32[8,128]{1,0:T(8,128)}, /*index=5*/f32[32,3,8,384]{3,2,1,0:T(8,128)}) custom-call(bf16[2880,128]{1,0:T(8,128)(2,1)} %bitcast.23, bf16[32,2880]{1,0:T(8,128)(2,1)} %bitcast.25, f32[1,32]{1,0:T(1,128)} %bitcast.28, ...), custom_call_target="tpu_custom_call" | custom-call | tf_op jit(solution)/shard_map/whole/pallas_call | solution.py:630
  136.4 5.1 %finish.1 = (bf16[128,1536]{1,0:T(8,128)(2,1)}, bf16[128,4,1536]{2,1,0:T(4,128)(2,1)}, bf16[2880,128]{1,0:T(8,128)(2,1)}, f32[32,3,8,384]{3,2,1,0:T(8,128)}, f32...) custom-call(bf16[128,1536]{1,0:T(8,128)(2,1)} %get-tuple-element.20.mixed, ...), custom_call_target="tpu_custom_call" | custom-call | tf_op jit(solution)/shard_map/finish/pallas_call | solution.py:599
